TPU v7x, 512 devices: a whole 4x4x16 slice. The times are simulated.
512 devices in a mesh: date: 64 (over z_lo, y, core), az: 8 (over z_hi, x).
Axes of the slice: x: 4, y: 4, z: 16 (z_hi: 2, z_lo: 8; z = z_hi * 8 + z_lo), core: 2. Of those that a mesh axis runs over, the one named last changes fastest.
Arguments:
- images: float32 [2, 64, 1024, 128], P(None, 'date', 'az'), may hold values from -12 to 12
- shifts: int32 [64, 2], P('date'), may hold values from -4 to 4, as said below
- fractions: int32 [64, 2], P('date'), may hold values from 0 to 15
- exponents: float32 [64], replicated, may hold values from 0.2 to 0.8
Outputs:
- filtered: float32 [2, 64, 1024, 128], P(None, 'date', 'az')
Inputs may be any that keep to these rules, and one draw needn't show every extreme that they name: `shifts`: in every draw some date has both offsets equal to 4 and another date has both equal to -4.
All inputs are finite; a program needn't handle non-finite values.
Results may differ from a plain program's by a relative error of at most 0.0027.
Values may be sent and summed in bfloat16 or wider, within the bound.
No kernel may reach another device: no remote copies, remote signals or barrier semaphores. Data moves between devices by JAX's collectives and lax.ppermute only.
A program may use at most 64 MiB of HBM per device.

v0:
```python
from functools import partial
import math

import jax
import jax.numpy as jnp
from jax import lax
from jax.sharding import PartitionSpec as P

PATCH = 16
HALF_WIN = 8
WIN = 17
TAPS = 8
FRAC = 16
REACH = 8
ITERS = 3


EPS = 1e-05
DAMP = 1.0


def padded_2(value, sides, width):
    for axis, dim in sides:
        size, length = (lax.axis_size(axis), value.shape[dim])
        up = [(i, (i + 1) % size) for i in range(size - 1)]
        down = [(j, i) for i, j in up]
        last = lax.slice_in_dim(value, length - width, length, axis=dim)
        initial = lax.slice_in_dim(value, 0, width, axis=dim)
        before = lax.ppermute(last, axis, up)
        after = lax.ppermute(initial, axis, down)
        value = jnp.concatenate([before, value, after], axis=dim)
    return value


def sinc_taps(fraction):
    offsets = jnp.arange(TAPS, dtype=jnp.float32) - (TAPS // 2 - 1)
    position = offsets - fraction.astype(jnp.float32) / FRAC
    window_weight = 0.5 + 0.5 * jnp.cos(2.0 * math.pi * position / TAPS)
    return jnp.sinc(position) * window_weight


def apply_taps(source, weights, displacement, axis_number, extent):
    opening = REACH + displacement - (TAPS // 2 - 1)
    window_part = lax.dynamic_slice_in_dim(source, opening, extent + TAPS - 1, axis_number)
    summed = weights[0] * lax.slice_in_dim(window_part, 0, extent, axis=axis_number)
    for tap_index in range(1, TAPS):
        summed = summed + weights[tap_index] * lax.slice_in_dim(
            window_part, tap_index, tap_index + extent, axis=axis_number
        )
    return summed


def resample_block(extended, shift_pair, fraction_pair, extent):
    padded = jnp.pad(extended, ((0, 0), (0, 0), (REACH, REACH)))
    by_rows = apply_taps(padded, sinc_taps(fraction_pair[0]), shift_pair[0], 1, extent)
    return apply_taps(by_rows, sinc_taps(fraction_pair[1]), shift_pair[1], 2, extended.shape[2])


def apply_matrix(matrix, vector):
    return jnp.einsum("pmn,pn->pm", matrix, vector, precision=lax.Precision.HIGHEST)


def power_link(moment):
    count_dates = moment.shape[-1] // 2
    real_part = moment[:, :count_dates, :count_dates] + moment[:, count_dates:, count_dates:]
    imag_part = moment[:, count_dates:, :count_dates] - moment[:, :count_dates, count_dates:]
    diagonal_power = jnp.diagonal(real_part, axis1=1, axis2=2)
    scaling = lax.rsqrt(diagonal_power / (WIN * WIN) + EPS)
    outer_scale = scaling[:, :, None] * scaling[:, None, :] / (WIN * WIN)
    gamma_real = real_part * outer_scale
    gamma_imag = imag_part * outer_scale
    vector_real = jnp.ones(diagonal_power.shape, jnp.float32)
    vector_imag = jnp.zeros(diagonal_power.shape, jnp.float32)
    for iteration in range(ITERS):
        new_real = (
            apply_matrix(gamma_real, vector_real)
            - apply_matrix(gamma_imag, vector_imag)
            + DAMP * vector_real
        )
        new_imag = (
            apply_matrix(gamma_real, vector_imag)
            + apply_matrix(gamma_imag, vector_real)
            + DAMP * vector_imag
        )
        inverse_norm = lax.rsqrt(
            jnp.sum(new_real * new_real + new_imag * new_imag, axis=1, keepdims=True) / count_dates
            + EPS
        )
        vector_real = new_real * inverse_norm
        vector_imag = new_imag * inverse_norm
    return (vector_real, vector_imag)


def link_tile(extended_tile):
    tile_rows = extended_tile.shape[0] - 2 * HALF_WIN
    tile_cols = extended_tile.shape[1] - 2 * HALF_WIN

    def one_row(row_index):
        window_rows = lax.dynamic_slice_in_dim(extended_tile, row_index, WIN, 0)
        patches = jnp.stack(
            [window_rows[:, column_lag : column_lag + tile_cols, :] for column_lag in range(WIN)],
            axis=0,
        )
        patches = patches.reshape((WIN * WIN, tile_cols, extended_tile.shape[2]))
        moment = jnp.einsum("wpk,wpl->pkl", patches, patches, preferred_element_type=jnp.float32)
        return power_link(moment)

    return lax.map(one_row, jnp.arange(tile_rows, dtype=jnp.int32))


def dft_tables(table_size):
    positions = jnp.arange(table_size, dtype=jnp.int32)
    same_block = positions[:, None] // PATCH == positions[None, :] // PATCH
    phase_index = positions[:, None] % PATCH * (positions[None, :] % PATCH) % PATCH
    angles = 2.0 * math.pi * phase_index.astype(jnp.float32) / PATCH
    table_real = jnp.where(same_block, jnp.cos(angles), 0.0) / math.sqrt(PATCH)
    table_imag = jnp.where(same_block, -jnp.sin(angles), 0.0) / math.sqrt(PATCH)
    return (table_real, table_imag)


def row_product(matrix, source):
    source_shape = source.shape
    blocked = source.reshape(
        source_shape[:-2] + (source_shape[-2] // PATCH, PATCH, source_shape[-1])
    )
    result = jnp.einsum("ij,...bjc->...bic", matrix, blocked, precision=lax.Precision.HIGHEST)
    return result.reshape(source_shape)


def column_product(source, matrix):
    return jnp.einsum("...c,cd->...d", source, matrix, precision=lax.Precision.HIGHEST)


def transform(source_real, source_imag, rows_real, rows_imag, cols_real, cols_imag):
    inner_real = row_product(rows_real, source_real) - row_product(rows_imag, source_imag)
    inner_imag = row_product(rows_real, source_imag) + row_product(rows_imag, source_real)
    outer_real = column_product(inner_real, cols_real) - column_product(inner_imag, cols_imag)
    outer_imag = column_product(inner_real, cols_imag) + column_product(inner_imag, cols_real)
    return (outer_real, outer_imag)


def patch_filter(field_real, field_imag, exponent):
    rows_real, rows_imag = dft_tables(PATCH)
    cols_real, cols_imag = dft_tables(field_real.shape[-1])
    spectrum_real, spectrum_imag = transform(
        field_real, field_imag, rows_real, rows_imag, cols_real, cols_imag
    )
    weighting = jnp.exp(
        exponent * jnp.log1p(spectrum_real * spectrum_real + spectrum_imag * spectrum_imag)
    )
    return transform(
        spectrum_real * weighting,
        spectrum_imag * weighting,
        rows_real,
        -rows_imag,
        cols_real,
        -cols_imag,
    )


def local(images, shifts, fractions, exponents):
    block_rows = images.shape[2]
    column_total = images.shape[3]
    az_count = lax.axis_size("az")
    date_count = lax.axis_size("date")
    tile_rows = block_rows * az_count // date_count
    tile_cols = column_total // az_count
    extended = padded_2(images, (("az", 2),), REACH)
    resampled = jax.vmap(partial(resample_block, extent=block_rows), in_axes=(1, 0, 0), out_axes=1)(
        extended, shifts, fractions
    )
    samples = resampled.astype(jnp.bfloat16)
    arrived = lax.all_to_all(
        lax.all_to_all(samples, "az", split_axis=3, concat_axis=2, tiled=True),
        "date",
        split_axis=2,
        concat_axis=1,
        tiled=True,
    )
    planes = arrived.reshape((2 * arrived.shape[1], tile_rows, tile_cols))
    tile_samples = jnp.transpose(planes, (1, 2, 0))
    extended_tile = padded_2(tile_samples, (("date", 0), ("az", 1)), HALF_WIN)
    vector_real, vector_imag = link_tile(extended_tile)
    linked = jnp.transpose(jnp.stack([vector_real, vector_imag]), (0, 3, 1, 2))
    returned = lax.all_to_all(
        lax.all_to_all(linked, "date", split_axis=1, concat_axis=2, tiled=True),
        "az",
        split_axis=2,
        concat_axis=3,
        tiled=True,
    )
    local_dates = returned.shape[1]
    own_exponents = lax.dynamic_slice_in_dim(
        exponents, lax.axis_index("date") * local_dates, local_dates, 0
    )
    return jnp.stack(patch_filter(returned[0], returned[1], own_exponents[:, None, None]))


def solution(mesh):
    return jax.shard_map(
        local,
        mesh=mesh,
        in_specs=(P(None, "date", "az", None), P("date", None), P("date", None), P()),
        out_specs=P(None, "date", "az", None),
        check_vma=False,
    )
```

profile of v0, /device:TPU:7, one launch (start us, length us, event | category | flops | bytes accessed | tf_op | source)
XLA Modules:
  0.0 540.8 jit_solution(18279196984114471200)
XLA Ops:
  0.7 15.3 %collective-permute-start = (f32[2,1,8,128]{3,2,1,0:T(8,128)S(1)}, f32[2,1,8,128]{3,2,1,0:T(8,128)S(1)}, u32[]{:S(2)}, u32[]{:S(2)}) collective-permute-start(f32[2,1,8,128]{3,2,1,0:T(8,128)S(1)} %get-tuple-element.97), channel_id=1, source_target_pairs={{0,1},{1,2},{2,3},{3,4},{4,5},{5,6},{6,7},{8,9},{9,10},{10,11},{11... | collective-permute-start | bytes 24584 | tf_op jit(solution)/shard_map/ppermute | solution.py:29
  25.9 5.4 collective-permute-done.1
  32.4 2.9 multiply_add_fusion
  35.3 3.3 fusion.43
  38.6 5.3 fusion.63
  43.9 20.4 %all_to_all.54 = bf16[2,1,128,128]{2,0,1,3:T(2,128)(2,1)S(1)} all-to-all(bf16[2,1,128,128]{2,0,1,3:T(2,128)(2,1)S(1)} %fusion.63), channel_id=1, replica_groups=mesh['date'=64,'az'=8] {'az'}, dimensions={3} | all-to-all | bytes 131072 | tf_op jit(solution)/shard_map/all_to_all | solution.py:174
  65.2 23.5 %all_to_all.55 = bf16[64,2,256]{2,1,0:T(2,128)(2,1)S(1)} all-to-all(bf16[64,2,256]{2,1,0:T(2,128)(2,1)S(1)} %reshape.609), channel_id=1, replica_groups=mesh['date'=64,'az'=8] {'date'}, dimensions={0} | all-to-all | bytes 131072 | tf_op jit(solution)/shard_map/all_to_all | solution.py:173
  90.1 2.5 collective-permute-start.2
  94.7 4.0 collective-permute-done.2
  98.9 4.2 collective-permute-done.3
  103.3 3.8 collective-permute-start.4
  107.1 2.1 collective-permute-start.5
  109.2 13.7 %collective-permute-done.5 = bf16[32,8,128]{2,1,0:T(8,128)(2,1)S(1)} collective-permute-done((bf16[32,8,128]{2,1,0:T(8,128)(2,1)S(1)}, bf16[32,8,128]{2,1,0:T(8,128)(2,1)S(1)}, u32[]{:S(2)}, u32[]{:S(2)}) %collective-permute-start.5) | collective-permute-done | bytes 65568 | tf_op jit(solution)/shard_map/ppermute | solution.py:30
  123.0 358.1 %while.14 = (s32[]{:T(128)}, f32[16,16,64]{2,1,0:T(8,128)}, f32[16,16,64]{2,1,0:T(8,128)}, s32[16]{0:T(128)S(1)}, bf16[32,32,128]{2,1,0:T(8,128)(2,1)S(1)}, /*in...) while((s32[]{:T(128)}, f32[16,16,64]{2,1,0:T(8,128)}, ...), condition=%wide.region_4.6_spmd, body=%wide.region_0.5_spmd.sunk | while | flops 162506048 | bytes 11754107 | solution.py:108
  130.9 2.1 fusion.390
  153.3 2.1 fusion.390
  175.7 2.1 fusion.390
  198.1 2.1 fusion.390
  220.4 2.1 fusion.390
  354.7 2.1 fusion.390
  483.5 24.6 %all_to_all.56 = f32[64,1,512]{2,1,0:T(1,128)S(1)} all-to-all(f32[64,1,512]{2,1,0:T(1,128)S(1)} %reshape.611), channel_id=1, replica_groups=mesh['date'=64,'az'=8] {'date'}, dimensions={0} | all-to-all | bytes 262144 | tf_op jit(solution)/shard_map/all_to_all | solution.py:186
  510.4 2.1 reshape.613
  512.5 3.9 all-to-all-start.3
  517.1 11.9 %all-to-all-done.3 = f32[8,1,4096]{2,1,0:T(1,128)S(1)} async-done(((f32[8,1,4096]{2,1,0:T(1,128)}), f32[8,1,4096]{2,1,0:T(1,128)S(1)}, u32[]{:S(2)}, u32[]{:S(2)}) %all-to-all-start.3) | async-done | bytes 131104 | tf_op jit(solution)/shard_map/all_to_all | solution.py:185
  (877 shorter events, 342.4 us)
Async XLA Ops:
  0.7 25.2 %collective-permute-start = (f32[2,1,8,128]{3,2,1,0:T(8,128)S(1)}, f32[2,1,8,128]{3,2,1,0:T(8,128)S(1)}, u32[]{:S(2)}, u32[]{:S(2)}) collective-permute-start(f32[2,1,8,128]{3,2,1,0:T(8,128)S(1)} %get-tuple-element.97), channel_id=1, source_target_pairs={{0,1},{1,2},{2,3},{3,4},{4,5},{5,6},{6,7},{8,9},{9,10},{10,11},{11... | collective-permute-start | bytes 24584 | tf_op jit(solution)/shard_map/ppermute | solution.py:29
  16.1 15.2 %collective-permute-start.1 = (f32[2,1,8,128]{3,2,1,0:T(8,128)S(1)}, f32[2,1,8,128]{3,2,1,0:T(8,128)S(1)}, u32[]{:S(2)}, u32[]{:S(2)}) collective-permute-start(f32[2,1,8,128]{3,2,1,0:T(8,128)S(1)} %get-tuple-element.96), channel_id=1, source_target_pairs={{1,0},{2,1},{3,2},{4,3},{5,4},{6,5},{7,6},{9,8},{10,9},{11,10},{12... | collective-permute-start | bytes 24584 | tf_op jit(solution)/shard_map/ppermute | solution.py:30
  90.1 8.6 %collective-permute-start.2 = (bf16[8,16,128]{0,2,1:T(8,128)(2,1)S(1)}, bf16[8,16,128]{0,2,1:T(8,128)(2,1)S(1)}, u32[]{:S(2)}, u32[]{:S(2)}) collective-permute-start(bf16[8,16,128]{0,2,1:T(8,128)(2,1)S(1)} %get-tuple-element.81), channel_id=1, source_target_pairs={{0,8},{8,16},{16,24},{24,32},{32,40},{40,48},{48,56},{56,64},{64,7... | collective-permute-start | bytes 98312 | tf_op jit(solution)/shard_map/ppermute | solution.py:29
  92.6 10.5 %collective-permute-start.3 = (bf16[8,16,128]{0,2,1:T(8,128)(2,1)S(1)}, bf16[8,16,128]{0,2,1:T(8,128)(2,1)S(1)}, u32[]{:S(2)}, u32[]{:S(2)}) collective-permute-start(bf16[8,16,128]{0,2,1:T(8,128)(2,1)S(1)} %get-tuple-element.82), channel_id=1, source_target_pairs={{8,0},{16,8},{24,16},{32,24},{40,32},{48,40},{56,48},{64,56},{72,6... | collective-permute-start | bytes 98312 | tf_op jit(solution)/shard_map/ppermute | solution.py:30
  103.3 5.9 %collective-permute-start.4 = (bf16[32,8,128]{2,1,0:T(8,128)(2,1)S(1)}, bf16[32,8,128]{2,1,0:T(8,128)(2,1)S(1)}, u32[]{:S(2)}, u32[]{:S(2)}) collective-permute-start(bf16[32,8,128]{2,1,0:T(8,128)(2,1)S(1)} %get-tuple-element.94), channel_id=1, source_target_pairs={{0,1},{1,2},{2,3},{3,4},{4,5},{5,6},{6,7},{8,9},{9,10},{10,11},{11... | collective-permute-start | bytes 196616 | tf_op jit(solution)/shard_map/ppermute | solution.py:29
  107.1 15.8 %collective-permute-start.5 = (bf16[32,8,128]{2,1,0:T(8,128)(2,1)S(1)}, bf16[32,8,128]{2,1,0:T(8,128)(2,1)S(1)}, u32[]{:S(2)}, u32[]{:S(2)}) collective-permute-start(bf16[32,8,128]{2,1,0:T(8,128)(2,1)S(1)} %get-tuple-element.95), channel_id=1, source_target_pairs={{1,0},{2,1},{3,2},{4,3},{5,4},{6,5},{7,6},{9,8},{10,9},{11,10},{12... | collective-permute-start | bytes 196616 | tf_op jit(solution)/shard_map/ppermute | solution.py:30
  133.0 2.2 copy-start
  155.4 2.2 copy-start
  177.7 2.2 copy-start
  200.1 2.2 copy-start
  222.5 2.2 copy-start
  244.9 2.2 copy-start
  267.3 2.2 copy-start
  289.6 2.2 copy-start
  312.0 2.2 copy-start
  334.4 2.2 copy-start
  356.8 2.2 copy-start
  379.1 2.2 copy-start
  401.5 2.2 copy-start
  423.9 2.2 copy-start
  446.3 2.2 copy-start
  468.7 2.2 copy-start
  510.4 6.1 %copy-start.1 = (f32[64]{0:T(128)S(1)}, f32[64]{0:T(128)}, u32[]{:S(2)}) copy-start(f32[64]{0:T(128)} %param.10) | copy-start | bytes 772
  512.5 16.5 %all-to-all-start.3 = ((f32[8,1,4096]{2,1,0:T(1,128)}), f32[8,1,4096]{2,1,0:T(1,128)S(1)}, u32[]{:S(2)}, u32[]{:S(2)}) async-start(f32[8,1,4096]{2,1,0:T(1,128)} %reshape.613), calls=%async_computation.3 | async-start | bytes 262144 | tf_op jit(solution)/shard_map/all_to_all | solution.py:185
where the time goes:
time: 548 us; the launch traced here: 541 us
  matrix products  228 us (42%)
  local copies, waits for them, and re-layouts  78.2 us (14%)
  blocking collectives  68.5 us (12%)
  other arithmetic  58 us (11%)
  waiting for transfers between devices  39.2 us (7%)
  loops' own time  32.8 us (6%)
  starting transfers between devices  31.5 us (6%)
    dot_general x192, matrix products, apply_matrix(): jnp.einsum('pmn,pn->pm', matrix, vector, precision=lax.Precision.HIGHEST)  205 us
    another operation x1, loops' own time, link_tile(): return lax.map(one_row, jnp.arange(tile_rows, dtype=jnp.int32))  32.8 us
    add x16, local copies, waits for them, and re-layouts, power_link(): moment[:, :count_dates, :count_dates]  26.7 us
    all_to_all x1, blocking collectives, local(): lax.all_to_all(linked, 'date', split_axis=1, concat_axis=2, tiled=True)  24.6 us
    all_to_all x1, blocking collectives, local(): lax.all_to_all(lax.all_to_all(samples, 'az', split_axis=3, concat_axis=2,...  23.5 us
    ppermute x3, waiting for transfers between devices, padded_2(): after = lax.ppermute(initial, axis, down)  23.3 us
    ppermute x3, starting transfers between devices, padded_2(): before = lax.ppermute(last, axis, up)  21.6 us
    all_to_all x1, blocking collectives, local(): lax.all_to_all(samples, 'az', split_axis=3, concat_axis=2, tiled=True)  20.4 us
  transfers between devices with their start and end apart: 7, of which 5 were waited for; matrix products, arithmetic and copies ran while one was open for 1% of the time, Pallas kernels for 0%

commit v1 on v0

v1 whole, which is shorter than its diff:
```python
import math

import jax
import jax.numpy as jnp
import numpy as np
from jax import lax
from jax.experimental import pallas as pl
from jax.experimental.pallas import tpu as pltpu
from jax.sharding import PartitionSpec as P

PATCH = 16
HALF_WIN = 8
WIN = 17
TAPS = 8
FRAC = 16
REACH = 8
ITERS = 3
EPS = 1e-05
DAMP = 1.0

TILE = 16
SPAN = TILE + 2 * HALF_WIN
HALO = REACH + HALF_WIN
LANES = 128
GROUPS = LANES // SPAN
AREA = float(WIN * WIN)
LIMIT = 24 * 1024 * 1024

VMEM = pltpu.VMEM
SMEM = pltpu.SMEM
F32 = jnp.float32
BF16 = jnp.bfloat16


def tap_table():
    fraction = np.arange(FRAC, dtype=np.float64)[:, None] / FRAC
    position = np.arange(TAPS, dtype=np.float64)[None, :] - (TAPS // 2 - 1) - fraction
    window = 0.5 + 0.5 * np.cos(2.0 * math.pi * position / TAPS)
    return (np.sinc(position) * window).astype(np.float32)


def patch_transform():
    place = np.arange(TILE * TILE)
    rows, cols = place // TILE, place % TILE
    phase = (rows[:, None] * rows[None, :] + cols[:, None] * cols[None, :]) % PATCH
    angle = 2.0 * math.pi * phase / PATCH
    parts = []
    for full in (np.cos(angle) / PATCH, -np.sin(angle) / PATCH):
        high = full.astype(jnp.bfloat16)
        low = (full - high.astype(np.float64)).astype(jnp.bfloat16)
        parts += [high, low]
    return np.stack(parts)


def iota(shape, dim):
    return lax.broadcasted_iota(jnp.int32, shape, dim)


def split(value):
    high = value.astype(BF16)
    return high, (value - high.astype(F32)).astype(BF16)


def dot(a, b):
    return jnp.dot(a, b, preferred_element_type=F32)


def resample_kernel(
    last_block, shift_ref, fraction_ref, table_ref, block_ref, own_ref, before_ref, after_ref,
    out_ref, extended, rolled,
):
    rows = own_ref.shape[2]
    kept = rows + 2 * HALF_WIN
    shape = (kept, LANES)
    row_shift, col_shift = shift_ref[0, 0], shift_ref[0, 1]
    row_taps = [table_ref[fraction_ref[0, 0], tap] for tap in range(TAPS)]
    col_taps = [table_ref[fraction_ref[0, 1], tap] for tap in range(TAPS)]
    block = block_ref[0]
    row_at = iota(shape, 0)
    inside = jnp.logical_and(
        jnp.logical_or(block > 0, row_at >= HALF_WIN),
        jnp.logical_or(block < last_block, row_at < rows + HALF_WIN),
    )
    source = iota(shape, 1) + (col_shift - (TAPS // 2 - 1))
    turn = TAPS // 2 - 1 + LANES - col_shift
    for plane in range(2):
        extended[plane, 0:HALO] = before_ref[plane, 0]
        extended[plane, HALO : HALO + rows] = own_ref[plane, 0]
        extended[plane, HALO + rows : 2 * HALO + rows] = after_ref[plane, 0]
        opening = HALO - HALF_WIN - (TAPS // 2 - 1) + row_shift
        along = row_taps[0] * extended[plane, pl.ds(opening, kept), :]
        for tap in range(1, TAPS):
            along = along + row_taps[tap] * extended[plane, pl.ds(opening + tap, kept), :]
        total = None
        for tap in range(TAPS):
            moved = pltpu.roll(along, lax.rem(turn - tap, LANES), 1)
            at = source + tap
            moved = jnp.where(jnp.logical_and(at >= 0, at < LANES), moved, 0.0)
            total = col_taps[tap] * moved if tap == 0 else total + col_taps[tap] * moved
        total = jnp.where(inside, total, 0.0)
        for turn_step in range(LANES // TILE):
            rolled[turn_step, plane] = pltpu.roll(total, HALF_WIN + TILE * turn_step, 1)
    lane = iota((8, LANES), 1)
    group = lane // SPAN
    place = lane % SPAN
    tile_cols = LANES // TILE
    for tile_row in range(rows // TILE):
        for tile_col in range(tile_cols):
            planes = []
            for plane in range(2):
                tile = None
                for part in reversed(range(GROUPS)):
                    start = (2 * tile_row + part) * 8
                    piece = rolled[(2 * part - tile_col) % tile_cols, plane, start : start + 8, :]
                    tile = piece if tile is None else jnp.where(group == part, piece, tile)
                if tile_col == 0:
                    tile = jnp.where(place >= HALF_WIN, tile, 0.0)
                if tile_col == tile_cols - 1:
                    tile = jnp.where(place < HALF_WIN + TILE, tile, 0.0)
                planes.append(tile)
            both = jnp.concatenate(planes, axis=0)
            out_ref[tile_row * tile_cols + tile_col] = both.astype(BF16)


def resample(last_block, shifts, fractions, block, own, before, after):
    rows = own.shape[2]
    tiles = (rows // TILE) * (LANES // TILE)
    kept = rows + 2 * HALF_WIN
    smem = pl.BlockSpec(memory_space=SMEM)
    vmem = pl.BlockSpec(memory_space=VMEM)
    return pl.pallas_call(
        lambda *refs: resample_kernel(last_block, *refs),
        out_shape=jax.ShapeDtypeStruct((tiles, 2 * 8, LANES), BF16),
        in_specs=[smem] * 4 + [vmem] * 3,
        out_specs=vmem,
        scratch_shapes=[
            VMEM((2, rows + 2 * HALO, LANES), F32),
            VMEM((LANES // TILE, 2, kept, LANES), F32),
        ],
        compiler_params=pltpu.CompilerParams(vmem_limit_bytes=LIMIT),
        name="resample",
    )(shifts, fractions, tap_table(), block, own, before, after)


def link_kernel(
    tile_ref, exponent_ref, transform_ref, out_ref,
    loose, planes, pixels, mask, power, weights, vector,
):
    dates = tile_ref.shape[0]
    count = 2 * dates
    inner = TILE * TILE
    blocks = SPAN * SPAN // LANES
    loose[...] = tile_ref[...].astype(F32).reshape(loose.shape)
    at = iota((LANES, inner), 0)
    pixel = iota((LANES, inner), 1)
    col_lag = at % SPAN - pixel % TILE
    col_ok = jnp.logical_and(col_lag >= 0, col_lag < WIN)
    row_base = (at // SPAN) * 8 - pixel // TILE
    for b in range(blocks):
        here = slice(b * LANES, (b + 1) * LANES)
        real = loose[pl.ds(b, dates, stride=2 * blocks), :]
        imag = loose[pl.ds(blocks + b, dates, stride=2 * blocks), :]
        both = jnp.concatenate([real, imag], axis=0)
        planes[:, here] = both.astype(BF16)
        turned = both.T.astype(BF16)
        pixels[here, 0:count] = turned
        pixels[here, count : 2 * count] = turned
        high, low = split(real * real + imag * imag)
        power[0:dates, here] = high
        power[dates:count, here] = low
        row_lag = row_base + b
        ok = jnp.logical_and(col_ok, jnp.logical_and(row_lag >= 0, row_lag < WIN))
        mask[here, :] = jnp.where(ok, 1.0, 0.0)
    sums = dot(power[...], mask[...].astype(BF16))
    scaling = lax.rsqrt((sums[:dates] + sums[dates:]) / AREA + EPS)
    vector[0] = jnp.ones((dates, inner), F32)
    vector[1] = jnp.zeros((dates, inner), F32)

    def iterate(_, carry):
        real, imag = vector[0], vector[1]
        scaled_real, scaled_imag = scaling * real, scaling * imag
        rh, rl = split(scaled_real)
        ih, il = split(scaled_imag)
        weights[0:dates, 0:inner] = rh
        weights[0:dates, inner:] = ih
        weights[dates:count, 0:inner] = ih
        weights[dates:count, inner:] = -rh
        weights[count : count + dates, 0:inner] = rl
        weights[count : count + dates, inner:] = il
        weights[count + dates :, 0:inner] = il
        weights[count + dates :, inner:] = -rl
        total = jnp.zeros((count, 2 * inner), F32)
        step = 256
        for first in range(0, SPAN * SPAN, step):
            here = slice(first, first + step)
            inner_products = dot(pixels[here, :], weights[...])
            keep = mask[here, :]
            high, low = split(inner_products * jnp.concatenate([keep, keep], axis=1))
            total = total + dot(planes[:, here], high) + dot(planes[:, here], low)
        factor = scaling / AREA
        new_real = factor * (total[:dates, :inner] - total[dates:, inner:]) + DAMP * real
        new_imag = factor * (total[:dates, inner:] + total[dates:, :inner]) + DAMP * imag
        square = jnp.sum(new_real * new_real + new_imag * new_imag, axis=0, keepdims=True)
        inverse = lax.rsqrt(square / dates + EPS)
        vector[0] = new_real * inverse
        vector[1] = new_imag * inverse
        return carry

    lax.fori_loop(0, ITERS, iterate, 0)

    def transform(real, imag, sign):
        high, low = split(jnp.concatenate([real, imag], axis=0))
        stacked = jnp.concatenate([high, low], axis=0)
        cos = dot(stacked, transform_ref[0]) + dot(stacked, transform_ref[1])
        sin = dot(stacked, transform_ref[2]) + dot(stacked, transform_ref[3])
        cos = cos[:count] + cos[count:]
        sin = sign * (sin[:count] + sin[count:])
        return cos[:dates] - sin[dates:], sin[:dates] + cos[dates:]

    spectrum_real, spectrum_imag = transform(vector[0], vector[1], 1.0)
    square_shape = (dates, dates)
    own = jnp.where(iota(square_shape, 0) == iota(square_shape, 1), exponent_ref[...], 0.0)
    exponent = jnp.sum(own, axis=1, keepdims=True)
    size = spectrum_real * spectrum_real + spectrum_imag * spectrum_imag
    weighting = jnp.exp(exponent * jnp.log1p(size))
    real, imag = transform(spectrum_real * weighting, spectrum_imag * weighting, -1.0)
    out_ref[:, 0:inner] = real.astype(out_ref.dtype)
    out_ref[:, inner:] = imag.astype(out_ref.dtype)


def link(tile, exponents):
    dates = tile.shape[0]
    inner = TILE * TILE
    outer = SPAN * SPAN
    vmem = pl.BlockSpec(memory_space=VMEM)
    return pl.pallas_call(
        link_kernel,
        out_shape=jax.ShapeDtypeStruct((dates, 2 * inner), BF16),
        in_specs=[vmem] * 3,
        out_specs=vmem,
        scratch_shapes=[
            VMEM((2 * dates * outer // LANES, LANES), F32),
            VMEM((2 * dates, outer), BF16),
            VMEM((outer, 4 * dates), BF16),
            VMEM((outer, inner), F32),
            VMEM((2 * dates, outer), BF16),
            VMEM((4 * dates, 2 * inner), BF16),
            VMEM((2, dates, inner), F32),
        ],
        compiler_params=pltpu.CompilerParams(vmem_limit_bytes=LIMIT),
        name="link",
    )(tile, exponents.reshape(1, dates), patch_transform())


def unpack_kernel(tile_ref, out_ref):
    tile_cols = LANES // TILE
    shape = (8, LANES)
    sub = iota(shape, 0)
    column = iota(shape, 1) // TILE
    halves = TILE // 8
    for tile_row in range(tile_ref.shape[0] // tile_cols):
        for plane in range(2):
            for half in range(halves):
                first = (plane * halves + half) * LANES
                value = tile_ref[
                    tile_row * tile_cols : (tile_row + 1) * tile_cols, first : first + LANES
                ].astype(F32)
                for step in (1, 2, 4):
                    ahead = pltpu.roll(pltpu.roll(value, 8 - step, 0), TILE * step, 1)
                    behind = pltpu.roll(pltpu.roll(value, step, 0), LANES - TILE * step, 1)
                    sub_bit = jnp.bitwise_and(sub, step) != 0
                    col_bit = jnp.bitwise_and(column, step) != 0
                    swapped = jnp.where(sub_bit, behind, ahead)
                    value = jnp.where(sub_bit == col_bit, value, swapped)
                row = tile_row * TILE + half * 8
                out_ref[plane, 0, row : row + 8, :] = value


def unpack(tiles):
    rows = tiles.shape[0] * TILE * TILE // LANES
    vmem = pl.BlockSpec(memory_space=VMEM)
    return pl.pallas_call(
        unpack_kernel,
        out_shape=jax.ShapeDtypeStruct((2, 1, rows, LANES), F32),
        in_specs=[vmem],
        out_specs=vmem,
        compiler_params=pltpu.CompilerParams(vmem_limit_bytes=LIMIT),
        name="unpack",
    )(tiles)


def local(images, shifts, fractions, exponents):
    rows = images.shape[2]
    blocks = lax.axis_size("az")
    up = [(i, i + 1) for i in range(blocks - 1)]
    down = [(j, i) for i, j in up]
    before = lax.ppermute(lax.slice_in_dim(images, rows - HALO, rows, axis=2), "az", up)
    after = lax.ppermute(lax.slice_in_dim(images, 0, HALO, axis=2), "az", down)
    block = lax.axis_index("az").astype(jnp.int32).reshape(1)
    packed = resample(blocks - 1, shifts, fractions, block, images, before, after)
    tile = lax.all_to_all(packed, "date", split_axis=0, concat_axis=0, tiled=True)
    filtered = link(tile, exponents)
    returned = lax.all_to_all(filtered, "date", split_axis=0, concat_axis=0, tiled=True)
    return unpack(returned)


def solution(mesh):
    return jax.shard_map(
        local,
        mesh=mesh,
        in_specs=(P(None, "date", "az", None), P("date", None), P("date", None), P()),
        out_specs=P(None, "date", "az", None),
        check_vma=False,
    )
```

time: 548 us -> 91.8 us (0.17); the launches traced: 541 us -> 91.5 us
  matrix products: 228 us -> 0 us
  local copies, waits for them, and re-layouts: 78.2 us -> 4.96 us
  other arithmetic: 58 us -> 0.66 us
  loops' own time: 32.8 us -> 0 us
  waiting for transfers between devices: 39.2 us -> 13.4 us
  blocking collectives: 68.5 us -> 48.5 us
  starting transfers between devices: 31.5 us -> 17.3 us
  Pallas kernels: 0 us -> 6.69 us
    dot_general x224 -> x0, matrix products: 228 us -> none  [the longest x192 205 us: apply_matrix(): jnp.einsum('pmn,pn->pm', matrix, vector, precision=lax.Precision.HIGHEST)]
    another operation x1 -> x0, loops' own time: 32.8 us -> none  [link_tile(): return lax.map(one_row, jnp.arange(tile_rows, dtype=jnp.int32))]
    add x16 -> x0, local copies, waits for them, and re-layouts: 26.7 us -> none  [power_link(): moment[:, :count_dates, :count_dates]]
    add x18 -> x0, other arithmetic: 22.4 us -> none  [the longest x16 16.2 us: power_link(): moment[:, :count_dates, :count_dates]]
    all_to_all x3 -> x2, blocking collectives: 68.5 us -> 48.5 us  [the longest x1 29.9 us: local(): lax.all_to_all(packed, 'date', split_axis=0, concat_axis=0, tiled=True)]
    gather x17 -> x0, local copies, waits for them, and re-layouts: 14.3 us -> none  [the longest x16 14.1 us: power_link(): diagonal_power = jnp.diagonal(real_part, axis1=1, axis2=2)]
    ppermute x6 -> x2, waiting for transfers between devices: 27.2 us -> 13.4 us  [the longest x1 13.4 us: local(): after = lax.ppermute(lax.slice_in_dim(images, 0, HALO, axis=2), 'az', down)]
    all_to_all x1 -> x0, waiting for transfers between devices: 11.9 us -> none  [local(): lax.all_to_all(lax.all_to_all(linked, 'date', split_axis=1, concat_axis=2...]
  transfers between devices with their start and end apart: 7 -> 2, of which waited for: 5 -> 1; matrix products, arithmetic and copies ran while one was open for 1% -> 0% of each run, Pallas kernels for 0% -> 0%
where the time goes in v1:
time: 91.8 us; the launch traced here: 91.5 us
  blocking collectives  48.5 us (53%)
  starting transfers between devices  17.3 us (19%)
  waiting for transfers between devices  13.4 us (15%)
  Pallas kernels  6.69 us (7%)
  local copies, waits for them, and re-layouts  4.96 us (5%)
    all_to_all x1, blocking collectives, local(): lax.all_to_all(packed, 'date', split_axis=0, concat_axis=0, tiled=True)  29.9 us
    all_to_all x1, blocking collectives, local(): lax.all_to_all(filtered, 'date', split_axis=0, concat_axis=0, tiled=True)  18.6 us
    ppermute x1, starting transfers between devices, local(): lax.ppermute(lax.slice_in_dim(images, rows - HALO, rows, axis=2), 'az', up)  15.3 us
    ppermute x1, waiting for transfers between devices, local(): after = lax.ppermute(lax.slice_in_dim(images, 0, HALO, axis=2), 'az', down)  13.4 us
    pallas_call x1, Pallas kernels, link(): pl.pallas_call(link_kernel, out_shape=jax.ShapeDtypeStruct((dates, 2 * in...  4.37 us
    unnamed x15, local copies, waits for them, and re-layouts  3.65 us
    ppermute x1, starting transfers between devices, local(): after = lax.ppermute(lax.slice_in_dim(images, 0, HALO, axis=2), 'az', down)  1.92 us
  transfers between devices with their start and end apart: 2, of which 1 were waited for; matrix products, arithmetic and copies ran while one was open for 0% of the time, Pallas kernels for 0%

profile of v1, /device:TPU:7, one launch (start us, length us, event | category | flops | bytes accessed | tf_op | source)
XLA Modules:
  0.0 91.5 jit_solution(10494882209529057463)
XLA Ops:
  0.0 0.0 copy-start
  0.0 0.8 fusion
  0.8 15.3 %collective-permute-start = (f32[2,1,16,128]{3,2,1,0:T(8,128)S(1)}, f32[2,1,16,128]{3,2,1,0:T(8,128)S(1)}, u32[]{:S(2)}, u32[]{:S(2)}) collective-permute-start(f32[2,1,16,128]{3,2,1,0:T(8,128)S(1)} %get-tuple-element.6), channel_id=1, source_target_pairs={{0,1},{1,2},{2,3},{3,4},{4,5},{5,6},{6,7},{8,9},{9,10},{10,11},{11... | collective-permute-start | bytes 49160 | tf_op jit(solution)/shard_map/ppermute | solution.py:297
  16.2 1.9 %collective-permute-start.1 = (f32[2,1,16,128]{3,2,1,0:T(8,128)S(1)}, f32[2,1,16,128]{3,2,1,0:T(8,128)S(1)}, u32[]{:S(2)}, u32[]{:S(2)}) collective-permute-start(f32[2,1,16,128]{3,2,1,0:T(8,128)S(1)} %get-tuple-element.5), channel_id=1, source_target_pairs={{1,0},{2,1},{3,2},{4,3},{5,4},{6,5},{7,6},{9,8},{10,9},{11,10},{12... | collective-permute-start | bytes 49160 | tf_op jit(solution)/shard_map/ppermute | solution.py:298
  18.1 0.0 collective-permute-done.refs_5_
  18.1 13.4 %collective-permute-done.1.refs_6_ = f32[2,1,16,128]{3,2,1,0:T(8,128)S(1)} collective-permute-done((f32[2,1,16,128]{3,2,1,0:T(8,128)S(1)}, f32[2,1,16,128]{3,2,1,0:T(8,128)S(1)}, u32[]{:S(2)}, u32[]{:S(2)}) %collective-permute-start.1) | collective-permute-done | bytes 16416 | tf_op jit(solution)/shard_map/ppermute | solution.py:298
  31.5 0.0 copy-start.1
  31.5 0.9 copy-done.1
  32.4 0.0 copy-start.2
  32.4 0.7 copy-done.2
  33.1 0.0 copy-start.3
  33.1 0.7 copy-done.3
  33.7 0.0 copy-start.4
  33.7 0.7 copy-done.4
  34.4 1.4 %resample.1 = bf16[64,16,128]{2,1,0:T(8,128)(2,1)S(1)} custom-call(s32[1,2]{1,0:T(1,128)S(1)} %copy-done.3, s32[1,2]{1,0:T(1,128)S(1)} %copy-done.4, f32[16,8]{1,0:T(8,128)S(1)} %copy-done.2, s32[1]{0:T(128)} %bitcast.refs_3_, f32[2,1,128,128]{3,2,1,0:T(8,128)S(1)} %copy-done.1, f32[2,1,16,128]{3,2,1,0:T(8,128)S(1)} %collective-permute-done.refs_5_, ...), custom_call_target="tpu_custom_call" | custom-call | tf_op jit(solution)/shard_map/resample/pallas_call | solution.py:131
  35.8 29.9 %all_to_all.16.tile_ref = bf16[64,16,128]{2,1,0:T(8,128)(2,1)S(1)} all-to-all(bf16[64,16,128]{2,1,0:T(8,128)(2,1)S(1)} %resample.1), channel_id=1, replica_groups=mesh['date'=64,'az'=8] {'date'}, dimensions={0} | all-to-all | bytes 524288 | tf_op jit(solution)/shard_map/all_to_all | solution.py:301
  65.7 0.0 copy-done
  65.7 0.7 copy-done.5
  66.4 4.4 %link.1 = bf16[64,512]{1,0:T(8,128)(2,1)S(1)} custom-call(bf16[64,16,128]{2,1,0:T(8,128)(2,1)S(1)} %all_to_all.16.tile_ref, f32[1,64]{1,0:T(1,128)S(1)} %bitcast.8, bf16[4,256,256]{2,1,0:T(8,128)(2,1)S(1)} %copy-done), custom_call_target="tpu_custom_call" | custom-call | tf_op jit(solution)/shard_map/link/pallas_call | solution.py:236
  70.8 0.5 broadcast
  71.3 0.7 reduce
  72.0 18.6 %all_to_all.17 = bf16[64,2,256]{2,1,0:T(2,128)(2,1)S(1)} all-to-all(bf16[64,2,256]{2,1,0:T(2,128)(2,1)S(1)} %reshape.10), channel_id=1, replica_groups=mesh['date'=64,'az'=8] {'date'}, dimensions={0} | all-to-all | bytes 131072 | tf_op jit(solution)/shard_map/all_to_all | solution.py:303
  90.5 0.1 reshape.11
  90.6 0.9 unpack.1
  (3 shorter events, 0.0 us)
Async XLA Ops:
  0.0 65.7 %copy-start = (bf16[4,256,256]{2,1,0:T(8,128)(2,1)S(1)}, bf16[4,256,256]{2,1,0:T(8,128)(2,1)}, u32[]{:S(2)}) copy-start(bf16[4,256,256]{2,1,0:T(8,128)(2,1)} %constant.9.clone.transform_ref) | copy-start | bytes 1572868
  0.8 17.3 %collective-permute-start = (f32[2,1,16,128]{3,2,1,0:T(8,128)S(1)}, f32[2,1,16,128]{3,2,1,0:T(8,128)S(1)}, u32[]{:S(2)}, u32[]{:S(2)}) collective-permute-start(f32[2,1,16,128]{3,2,1,0:T(8,128)S(1)} %get-tuple-element.6), channel_id=1, source_target_pairs={{0,1},{1,2},{2,3},{3,4},{4,5},{5,6},{6,7},{8,9},{9,10},{10,11},{11... | collective-permute-start | bytes 49160 | tf_op jit(solution)/shard_map/ppermute | solution.py:297
  16.2 15.3 %collective-permute-start.1 = (f32[2,1,16,128]{3,2,1,0:T(8,128)S(1)}, f32[2,1,16,128]{3,2,1,0:T(8,128)S(1)}, u32[]{:S(2)}, u32[]{:S(2)}) collective-permute-start(f32[2,1,16,128]{3,2,1,0:T(8,128)S(1)} %get-tuple-element.5), channel_id=1, source_target_pairs={{1,0},{2,1},{3,2},{4,3},{5,4},{6,5},{7,6},{9,8},{10,9},{11,10},{12... | collective-permute-start | bytes 49160 | tf_op jit(solution)/shard_map/ppermute | solution.py:298
  31.5 0.9 copy-start.1
  32.4 0.7 copy-start.2
  33.1 0.7 copy-start.3
  33.7 0.7 copy-start.4
  65.7 0.7 copy-start.5

commit v2 on v1

--- a/solution.py
+++ b/solution.py
@@ -65,54 +65,131 @@
     return jnp.dot(a, b, preferred_element_type=F32)
 
 
-def resample_kernel(
-    last_block, shift_ref, fraction_ref, table_ref, block_ref, own_ref, before_ref, after_ref,
-    out_ref, extended, rolled,
+def read_taps(shift_ref, fraction_ref, table_ref):
+    row_taps = [table_ref[fraction_ref[0, 0], tap] for tap in range(TAPS)]
+    col_taps = [table_ref[fraction_ref[0, 1], tap] for tap in range(TAPS)]
+    return shift_ref[0, 0], shift_ref[0, 1], row_taps, col_taps
+
+
+def filter_rows(source, opening, kept, taps):
+    along = taps[0] * source(opening, kept)
+    for tap in range(1, TAPS):
+        along = along + taps[tap] * source(opening + tap, kept)
+    return along
+
+
+def filter_cols(along, shift, taps):
+    at = iota(along.shape, 1) + (shift - (TAPS // 2 - 1))
+    turn = TAPS // 2 - 1 + LANES - shift
+    total = None
+    for tap in range(TAPS):
+        moved = pltpu.roll(along, lax.rem(turn - tap, LANES), 1)
+        here = at + tap
+        moved = jnp.where(jnp.logical_and(here >= 0, here < LANES), moved, 0.0)
+        total = taps[tap] * moved if tap == 0 else total + taps[tap] * moved
+    return total
+
+
+def inner_kernel(
+    shift_ref, fraction_ref, table_ref, own_ref, exponent_ref, rolled_ref, mask_ref, exponent_out_ref
+):
+    row_shift, col_shift, row_taps, col_taps = read_taps(shift_ref, fraction_ref, table_ref)
+    kept = own_ref.shape[2] - 2 * HALF_WIN
+    opening = HALF_WIN - (TAPS // 2 - 1) + row_shift
+    for plane in range(2):
+        along = filter_rows(
+            lambda first, size: own_ref[plane, 0, pl.ds(first, size), :], opening, kept, row_taps
+        )
+        total = filter_cols(along, col_shift, col_taps)
+        for turn in range(LANES // TILE):
+            rolled_ref[turn, plane] = pltpu.roll(total, HALF_WIN + TILE * turn, 1)
+    inner = TILE * TILE
+    at = iota((LANES, inner), 0)
+    pixel = iota((LANES, inner), 1)
+    col_lag = at % SPAN - pixel % TILE
+    col_ok = jnp.logical_and(col_lag >= 0, col_lag < WIN)
+    row_base = (at // SPAN) * 8 - pixel // TILE
+    for b in range(SPAN * SPAN // LANES):
+        row_lag = row_base + b
+        ok = jnp.logical_and(col_ok, jnp.logical_and(row_lag >= 0, row_lag < WIN))
+        mask_ref[b * LANES : (b + 1) * LANES, :] = jnp.where(ok, 1.0, 0.0).astype(BF16)
+    exponent_out_ref[...] = exponent_ref[...]
+
+
+def inner_resample(shifts, fractions, own, exponents):
+    rows = own.shape[2]
+    kept = rows - 2 * HALF_WIN
+    smem = pl.BlockSpec(memory_space=SMEM)
+    vmem = pl.BlockSpec(memory_space=VMEM)
+    return pl.pallas_call(
+        inner_kernel,
+        out_shape=(
+            jax.ShapeDtypeStruct((LANES // TILE, 2, kept, LANES), F32),
+            jax.ShapeDtypeStruct((SPAN * SPAN, TILE * TILE), BF16),
+            jax.ShapeDtypeStruct(exponents.shape, F32),
+        ),
+        in_specs=[smem] * 3 + [vmem] * 2,
+        out_specs=(vmem,) * 3,
+        compiler_params=pltpu.CompilerParams(vmem_limit_bytes=LIMIT),
+        cost_estimate=pl.CostEstimate(flops=2000000, bytes_accessed=2000000, transcendentals=0),
+        name="inner_resample",
+    )(shifts, fractions, tap_table(), own, exponents)
+
+
+def edge_kernel(
+    last_block, shift_ref, fraction_ref, table_ref, block_ref, own_ref, even_ref, odd_ref, rolled_ref,
+    out_ref, extended, edges,
 ):
     rows = own_ref.shape[2]
-    kept = rows + 2 * HALF_WIN
-    shape = (kept, LANES)
-    row_shift, col_shift = shift_ref[0, 0], shift_ref[0, 1]
-    row_taps = [table_ref[fraction_ref[0, 0], tap] for tap in range(TAPS)]
-    col_taps = [table_ref[fraction_ref[0, 1], tap] for tap in range(TAPS)]
+    row_shift, col_shift, row_taps, col_taps = read_taps(shift_ref, fraction_ref, table_ref)
     block = block_ref[0]
-    row_at = iota(shape, 0)
-    inside = jnp.logical_and(
-        jnp.logical_or(block > 0, row_at >= HALF_WIN),
-        jnp.logical_or(block < last_block, row_at < rows + HALF_WIN),
-    )
-    source = iota(shape, 1) + (col_shift - (TAPS // 2 - 1))
-    turn = TAPS // 2 - 1 + LANES - col_shift
-    for plane in range(2):
-        extended[plane, 0:HALO] = before_ref[plane, 0]
-        extended[plane, HALO : HALO + rows] = own_ref[plane, 0]
-        extended[plane, HALO + rows : 2 * HALO + rows] = after_ref[plane, 0]
-        opening = HALO - HALF_WIN - (TAPS // 2 - 1) + row_shift
-        along = row_taps[0] * extended[plane, pl.ds(opening, kept), :]
-        for tap in range(1, TAPS):
-            along = along + row_taps[tap] * extended[plane, pl.ds(opening + tap, kept), :]
-        total = None
-        for tap in range(TAPS):
-            moved = pltpu.roll(along, lax.rem(turn - tap, LANES), 1)
-            at = source + tap
-            moved = jnp.where(jnp.logical_and(at >= 0, at < LANES), moved, 0.0)
-            total = col_taps[tap] * moved if tap == 0 else total + col_taps[tap] * moved
-        total = jnp.where(inside, total, 0.0)
-        for turn_step in range(LANES // TILE):
-            rolled[turn_step, plane] = pltpu.roll(total, HALF_WIN + TILE * turn_step, 1)
+    is_even = lax.rem(block, 2) == 0
+    tile_cols = LANES // TILE
+    opening = HALO - HALF_WIN - (TAPS // 2 - 1) + row_shift
+    for side in range(2):
+        row_at = iota((HALO, LANES), 0)
+        if side == 0:
+            inside = jnp.logical_or(block > 0, row_at >= HALF_WIN)
+        else:
+            inside = jnp.logical_or(block < last_block, row_at < HALF_WIN)
+        for plane in range(2):
+            from_even = even_ref[plane, 0]
+            from_odd = odd_ref[plane, 0]
+            if side == 0:
+                extended[0:HALO] = jnp.where(is_even, from_odd, from_even)
+                extended[HALO : 2 * HALO] = own_ref[plane, 0, 0:HALO]
+            else:
+                extended[0:HALO] = own_ref[plane, 0, rows - HALO : rows]
+                extended[HALO : 2 * HALO] = jnp.where(is_even, from_even, from_odd)
+            along = filter_rows(
+                lambda first, size: extended[pl.ds(first, size), :], opening, HALO, row_taps
+            )
+            total = jnp.where(inside, filter_cols(along, col_shift, col_taps), 0.0)
+            for turn in range(tile_cols):
+                edges[turn, plane, side * HALO : (side + 1) * HALO] = pltpu.roll(
+                    total, HALF_WIN + TILE * turn, 1
+                )
+
+    def piece(turn, plane, step):
+        last = rows // 8 + 2
+        if step < 2:
+            return edges[turn, plane, step * 8 : step * 8 + 8, :]
+        if step >= last - 2:
+            start = HALO + (step - last + 2) * 8
+            return edges[turn, plane, start : start + 8, :]
+        return rolled_ref[turn, plane, (step - 2) * 8 : (step - 1) * 8, :]
+
     lane = iota((8, LANES), 1)
     group = lane // SPAN
     place = lane % SPAN
-    tile_cols = LANES // TILE
     for tile_row in range(rows // TILE):
         for tile_col in range(tile_cols):
             planes = []
             for plane in range(2):
                 tile = None
                 for part in reversed(range(GROUPS)):
-                    start = (2 * tile_row + part) * 8
-                    piece = rolled[(2 * part - tile_col) % tile_cols, plane, start : start + 8, :]
-                    tile = piece if tile is None else jnp.where(group == part, piece, tile)
+                    this = piece((2 * part - tile_col) % tile_cols, plane, 2 * tile_row + part)
+                    tile = this if tile is None else jnp.where(group == part, this, tile)
                 if tile_col == 0:
                     tile = jnp.where(place >= HALF_WIN, tile, 0.0)
                 if tile_col == tile_cols - 1:
@@ -122,40 +199,34 @@
             out_ref[tile_row * tile_cols + tile_col] = both.astype(BF16)
 
 
-def resample(last_block, shifts, fractions, block, own, before, after):
+def edge_resample(last_block, shifts, fractions, block, own, even, odd, rolled):
     rows = own.shape[2]
     tiles = (rows // TILE) * (LANES // TILE)
-    kept = rows + 2 * HALF_WIN
     smem = pl.BlockSpec(memory_space=SMEM)
     vmem = pl.BlockSpec(memory_space=VMEM)
     return pl.pallas_call(
-        lambda *refs: resample_kernel(last_block, *refs),
+        lambda *refs: edge_kernel(last_block, *refs),
         out_shape=jax.ShapeDtypeStruct((tiles, 2 * 8, LANES), BF16),
-        in_specs=[smem] * 4 + [vmem] * 3,
+        in_specs=[smem] * 4 + [vmem] * 4,
         out_specs=vmem,
         scratch_shapes=[
-            VMEM((2, rows + 2 * HALO, LANES), F32),
-            VMEM((LANES // TILE, 2, kept, LANES), F32),
+            VMEM((2 * HALO, LANES), F32),
+            VMEM((LANES // TILE, 2, 2 * HALO, LANES), F32),
         ],
         compiler_params=pltpu.CompilerParams(vmem_limit_bytes=LIMIT),
-        name="resample",
-    )(shifts, fractions, tap_table(), block, own, before, after)
+        name="edge_resample",
+    )(shifts, fractions, tap_table(), block, own, even, odd, rolled)
 
 
 def link_kernel(
-    tile_ref, exponent_ref, transform_ref, out_ref,
-    loose, planes, pixels, mask, power, weights, vector,
+    tile_ref, exponent_ref, transform_ref, mask, out_ref,
+    loose, planes, pixels, power, weights, vector,
 ):
     dates = tile_ref.shape[0]
     count = 2 * dates
     inner = TILE * TILE
     blocks = SPAN * SPAN // LANES
     loose[...] = tile_ref[...].astype(F32).reshape(loose.shape)
-    at = iota((LANES, inner), 0)
-    pixel = iota((LANES, inner), 1)
-    col_lag = at % SPAN - pixel % TILE
-    col_ok = jnp.logical_and(col_lag >= 0, col_lag < WIN)
-    row_base = (at // SPAN) * 8 - pixel // TILE
     for b in range(blocks):
         here = slice(b * LANES, (b + 1) * LANES)
         real = loose[pl.ds(b, dates, stride=2 * blocks), :]
@@ -168,10 +239,7 @@
         high, low = split(real * real + imag * imag)
         power[0:dates, here] = high
         power[dates:count, here] = low
-        row_lag = row_base + b
-        ok = jnp.logical_and(col_ok, jnp.logical_and(row_lag >= 0, row_lag < WIN))
-        mask[here, :] = jnp.where(ok, 1.0, 0.0)
-    sums = dot(power[...], mask[...].astype(BF16))
+    sums = dot(power[...], mask[...])
     scaling = lax.rsqrt((sums[:dates] + sums[dates:]) / AREA + EPS)
     vector[0] = jnp.ones((dates, inner), F32)
     vector[1] = jnp.zeros((dates, inner), F32)
@@ -194,7 +262,7 @@
         for first in range(0, SPAN * SPAN, step):
             here = slice(first, first + step)
             inner_products = dot(pixels[here, :], weights[...])
-            keep = mask[here, :]
+            keep = mask[here, :].astype(F32)
             high, low = split(inner_products * jnp.concatenate([keep, keep], axis=1))
             total = total + dot(planes[:, here], high) + dot(planes[:, here], low)
         factor = scaling / AREA
@@ -228,7 +296,7 @@
     out_ref[:, inner:] = imag.astype(out_ref.dtype)
 
 
-def link(tile, exponents):
+def link(tile, exponents, mask):
     dates = tile.shape[0]
     inner = TILE * TILE
     outer = SPAN * SPAN
@@ -236,20 +304,19 @@
     return pl.pallas_call(
         link_kernel,
         out_shape=jax.ShapeDtypeStruct((dates, 2 * inner), BF16),
-        in_specs=[vmem] * 3,
+        in_specs=[vmem] * 4,
         out_specs=vmem,
         scratch_shapes=[
             VMEM((2 * dates * outer // LANES, LANES), F32),
             VMEM((2 * dates, outer), BF16),
             VMEM((outer, 4 * dates), BF16),
-            VMEM((outer, inner), F32),
             VMEM((2 * dates, outer), BF16),
             VMEM((4 * dates, 2 * inner), BF16),
             VMEM((2, dates, inner), F32),
         ],
         compiler_params=pltpu.CompilerParams(vmem_limit_bytes=LIMIT),
         name="link",
-    )(tile, exponents.reshape(1, dates), patch_transform())
+    )(tile, exponents, patch_transform(), mask)
 
 
 def unpack_kernel(tile_ref, out_ref):
@@ -289,19 +356,32 @@
     )(tiles)
 
 
+def both_ways(boundaries):
+    return [(k, k + 1) for k in boundaries] + [(k + 1, k) for k in boundaries]
+
+
 def local(images, shifts, fractions, exponents):
     rows = images.shape[2]
     blocks = lax.axis_size("az")
-    up = [(i, i + 1) for i in range(blocks - 1)]
-    down = [(j, i) for i, j in up]
-    before = lax.ppermute(lax.slice_in_dim(images, rows - HALO, rows, axis=2), "az", up)
-    after = lax.ppermute(lax.slice_in_dim(images, 0, HALO, axis=2), "az", down)
-    block = lax.axis_index("az").astype(jnp.int32).reshape(1)
-    packed = resample(blocks - 1, shifts, fractions, block, images, before, after)
+    block = lax.axis_index("az").astype(jnp.int32)
+    first = lax.slice_in_dim(images, 0, HALO, axis=2)
+    last = lax.slice_in_dim(images, rows - HALO, rows, axis=2)
+    is_even = lax.rem(block, 2) == 0
+    to_odd = jnp.where(is_even, first, last)
+    to_even = jnp.where(is_even, last, first)
+    odd = lax.ppermute(to_odd, "az", both_ways(range(1, blocks - 1, 2)))
+    even = lax.ppermute(to_even, "az", both_ways(range(0, blocks - 1, 2)))
+    rolled, mask, exponent_row = inner_resample(
+        shifts, fractions, images, exponents.reshape(1, exponents.shape[0])
+    )
+    packed = edge_resample(
+        blocks - 1, shifts, fractions, block.reshape(1), images, even, odd, rolled
+    )
     tile = lax.all_to_all(packed, "date", split_axis=0, concat_axis=0, tiled=True)
-    filtered = link(tile, exponents)
+    filtered = link(tile, exponent_row, mask)
+    filtered = filtered.reshape(filtered.shape[0], -1, LANES)
     returned = lax.all_to_all(filtered, "date", split_axis=0, concat_axis=0, tiled=True)
-    return unpack(returned)
+    return unpack(returned.reshape(returned.shape[0], -1))
 
 
 def solution(mesh):

time: 91.8 us -> 78.3 us (0.85)
  waiting for transfers between devices: 13.4 us -> 0.01 us
  local copies, waits for them, and re-layouts: 4.96 us -> 0.96 us
  blocking collectives: 48.5 us -> 51 us
  Pallas kernels: 6.69 us -> 7.8 us
    ppermute x2, waiting for transfers between devices: 13.4 us -> 0.01 us  [the longest x1 0.01 us: local(): even = lax.ppermute(to_even, 'az', both_ways(range(0, blocks - 1, 2)))]
    unnamed x15 -> x13, local copies, waits for them, and re-layouts: 3.65 us -> 0.94 us
    all_to_all x1, blocking collectives: 29.9 us -> 32.4 us  [local(): lax.all_to_all(packed, 'date', split_axis=0, concat_axis=0, tiled=True)]
    pallas_call x1 -> x2, Pallas kernels: 1.4 us -> 2.68 us  [the longest x1 1.75 us: inner_resample(): pl.pallas_call(inner_kernel, out_shape=(jax.ShapeDtypeStruct((LANES // TI...]
  transfers between devices with their start and end apart: 2 -> 2, of which waited for: 1 -> 0; matrix products, arithmetic and copies ran while one was open for 0% -> 0% of each run, Pallas kernels for 0% -> 2%
where the time goes in v2:
time: 78.3 us; the launch traced here: 78 us
  blocking collectives  51 us (65%)
  starting transfers between devices  17.4 us (22%)
  Pallas kernels  7.8 us (10%)
  local copies, waits for them, and re-layouts  0.96 us (1%)
    all_to_all x1, blocking collectives, local(): lax.all_to_all(packed, 'date', split_axis=0, concat_axis=0, tiled=True)  32.4 us
    all_to_all x1, blocking collectives, local(): lax.all_to_all(filtered, 'date', split_axis=0, concat_axis=0, tiled=True)  18.6 us
    ppermute x1, starting transfers between devices, local(): odd = lax.ppermute(to_odd, 'az', both_ways(range(1, blocks - 1, 2)))  15.3 us
    pallas_call x1, Pallas kernels, link(): pl.pallas_call(link_kernel, out_shape=jax.ShapeDtypeStruct((dates, 2 * in...  4.22 us
    ppermute x1, starting transfers between devices, local(): even = lax.ppermute(to_even, 'az', both_ways(range(0, blocks - 1, 2)))  2.05 us
    pallas_call x1, Pallas kernels, inner_resample(): pl.pallas_call(inner_kernel, out_shape=(jax.ShapeDtypeStruct((LANES // TI...  1.75 us
  transfers between devices with their start and end apart: 2, of which 0 were waited for; matrix products, arithmetic and copies ran while one was open for 0% of the time, Pallas kernels for 2%

profile of v2, /device:TPU:7, one launch (start us, length us, event | category | flops | bytes accessed | tf_op | source)
XLA Modules:
  0.0 78.0 jit_solution(810149568568044466)
XLA Ops:
  0.0 0.0 copy-start.2
  0.0 0.8 slice_select_fusion
  0.8 15.3 %collective-permute-start.1 = (f32[2,1,16,128]{3,2,1,0:T(8,128)S(1)}, f32[2,1,16,128]{3,2,1,0:T(8,128)S(1)}, u32[]{:S(2)}, u32[]{:S(2)}) collective-permute-start(f32[2,1,16,128]{3,2,1,0:T(8,128)S(1)} %get-tuple-element.11), channel_id=1, source_target_pairs={{1,2},{3,4},{5,6},{2,1},{4,3},{6,5},{9,10},{11,12},{13,14},{10,9},... | collective-permute-start | bytes 49160 | tf_op jit(solution)/shard_map/ppermute | solution.py:372
  16.1 0.0 copy-start.3
  16.1 0.0 copy-start.4
  16.1 0.0 copy-start.5
  16.1 2.1 %collective-permute-start = (f32[2,1,16,128]{3,2,1,0:T(8,128)S(1)}, f32[2,1,16,128]{3,2,1,0:T(8,128)S(1)}, u32[]{:S(2)}, u32[]{:S(2)}) collective-permute-start(f32[2,1,16,128]{3,2,1,0:T(8,128)S(1)} %get-tuple-element.12), channel_id=1, source_target_pairs={{0,1},{2,3},{4,5},{6,7},{1,0},{3,2},{5,4},{7,6},{8,9},{10,11},{12,... | collective-permute-start | bytes 49160 | tf_op jit(solution)/shard_map/ppermute | solution.py:373
  18.2 0.0 copy-done.2
  18.2 0.0 copy-done.3
  18.2 0.0 copy-done.4
  18.2 0.0 copy-done.5
  18.2 0.0 copy-start
  18.3 0.9 %copy-done = f32[2,1,128,128]{3,2,1,0:T(8,128)S(1)} copy-done((f32[2,1,128,128]{3,2,1,0:T(8,128)S(1)}, f32[2,1,128,128]{3,2,1,0:T(8,128)}, u32[]{:S(2)}) %copy-start) | copy-done | bytes 131096
  19.2 1.7 %inner_resample.1 = (f32[8,2,112,128]{3,2,1,0:T(8,128)S(1)}, bf16[1024,256]{1,0:T(8,128)(2,1)S(1)}, f32[1,64]{1,0:T(1,128)S(1)}) custom-call(s32[1,2]{1,0:T(1,128)S(1)} %copy-done.3, s32[1,2]{1,0:T(1,128)S(1)} %copy-done.4, f32[16,8]{1,0:T(8,128)S(1)} %copy-done.2, f32[2,1,128,128]{3,2,1,0:T(8,128)S(1)} %copy-done, f32[1,64]{1,0:T(1,128)S(1)} %bitcast.7), custom_call_target="tpu_custom_call" | custom-call | flops 2000000 | bytes 2000000 | tf_op jit(solution)/shard_map/inner_resample/pallas_call | solution.py:124
  20.9 0.0 collective-permute-done.1.refs_6_
  20.9 0.0 collective-permute-done.refs_5_
  20.9 0.9 %edge_resample.1 = bf16[64,16,128]{2,1,0:T(8,128)(2,1)S(1)} custom-call(s32[1,2]{1,0:T(1,128)S(1)} %copy-done.3, s32[1,2]{1,0:T(1,128)S(1)} %copy-done.4, f32[16,8]{1,0:T(8,128)S(1)} %copy-done.2, s32[1]{0:T(128)} %bitcast.refs_3_, f32[2,1,128,128]{3,2,1,0:T(8,128)S(1)} %copy-done, f32[2,1,16,128]{3,2,1,0:T(8,128)S(1)} %collective-permute-done.refs_5_, ...), custom_call_target="tpu_custom_call" | custom-call | tf_op jit(solution)/shard_map/edge_resample/pallas_call | solution.py:207
  21.9 0.0 copy-start.1
  21.9 32.4 %all_to_all.10.tile_ref = bf16[64,16,128]{2,1,0:T(8,128)(2,1)S(1)} all-to-all(bf16[64,16,128]{2,1,0:T(8,128)(2,1)S(1)} %edge_resample.1), channel_id=1, replica_groups=mesh['date'=64,'az'=8] {'date'}, dimensions={0} | all-to-all | bytes 524288 | tf_op jit(solution)/shard_map/all_to_all | solution.py:380
  54.3 0.0 copy-done.1
  54.3 4.2 %link.1 = bf16[64,512]{1,0:T(8,128)(2,1)S(1)} custom-call(bf16[64,16,128]{2,1,0:T(8,128)(2,1)S(1)} %all_to_all.10.tile_ref, f32[1,64]{1,0:T(1,128)S(1)} %get-tuple-element.9.exponent_ref, bf16[4,256,256]{2,1,0:T(8,128)(2,1)S(1)} %copy-done.1, bf16[1024,256]{1,0:T(8,128)(2,1)S(1)} %get-tuple-element.10.mask), custom_call_target="tpu_custom_call" | custom-call | tf_op jit(solution)/shard_map/link/pallas_call | solution.py:304
  58.5 18.6 %all_to_all.11 = bf16[64,4,128]{2,1,0:T(4,128)(2,1)S(1)} all-to-all(bf16[64,4,128]{2,1,0:T(4,128)(2,1)S(1)} %reshape.14), channel_id=1, replica_groups=mesh['date'=64,'az'=8] {'date'}, dimensions={0} | all-to-all | bytes 131072 | tf_op jit(solution)/shard_map/all_to_all | solution.py:383
  77.1 0.9 %unpack.1 = f32[2,1,128,128]{3,2,1,0:T(8,128)} custom-call(bf16[64,512]{1,0:T(8,128)(2,1)S(1)} %bitcast.6), custom_call_target="tpu_custom_call" | custom-call | tf_op jit(solution)/shard_map/unpack/pallas_call | solution.py:349
  (2 shorter events, 0.0 us)
Async XLA Ops:
  0.0 18.2 %copy-start.2 = (f32[16,8]{1,0:T(8,128)S(1)}, f32[16,8]{1,0:T(8,128)}, u32[]{:S(2)}) copy-start(f32[16,8]{1,0:T(8,128)} %constant.14.clone.table_ref.refs_2_) | copy-start | bytes 1540
  0.8 20.2 %collective-permute-start.1 = (f32[2,1,16,128]{3,2,1,0:T(8,128)S(1)}, f32[2,1,16,128]{3,2,1,0:T(8,128)S(1)}, u32[]{:S(2)}, u32[]{:S(2)}) collective-permute-start(f32[2,1,16,128]{3,2,1,0:T(8,128)S(1)} %get-tuple-element.11), channel_id=1, source_target_pairs={{1,2},{3,4},{5,6},{2,1},{4,3},{6,5},{9,10},{11,12},{13,14},{10,9},... | collective-permute-start | bytes 49160 | tf_op jit(solution)/shard_map/ppermute | solution.py:372
  16.1 2.1 %copy-start.3 = (s32[1,2]{1,0:T(1,128)S(1)}, s32[1,2]{1,0:T(1,128)}, u32[]{:S(2)}) copy-start(s32[1,2]{1,0:T(1,128)} %refs_0_.1) | copy-start | bytes 28
  16.1 2.1 %copy-start.4 = (s32[1,2]{1,0:T(1,128)S(1)}, s32[1,2]{1,0:T(1,128)}, u32[]{:S(2)}) copy-start(s32[1,2]{1,0:T(1,128)} %refs_1_.1) | copy-start | bytes 28
  16.1 2.1 %copy-start.5 = (f32[64]{0:T(128)S(1)}, f32[64]{0:T(128)}, u32[]{:S(2)}) copy-start(f32[64]{0:T(128)} %param.10) | copy-start | bytes 772
  16.1 4.8 %collective-permute-start = (f32[2,1,16,128]{3,2,1,0:T(8,128)S(1)}, f32[2,1,16,128]{3,2,1,0:T(8,128)S(1)}, u32[]{:S(2)}, u32[]{:S(2)}) collective-permute-start(f32[2,1,16,128]{3,2,1,0:T(8,128)S(1)} %get-tuple-element.12), channel_id=1, source_target_pairs={{0,1},{2,3},{4,5},{6,7},{1,0},{3,2},{5,4},{7,6},{8,9},{10,11},{12,... | collective-permute-start | bytes 49160 | tf_op jit(solution)/shard_map/ppermute | solution.py:373
  18.2 0.9 %copy-start = (f32[2,1,128,128]{3,2,1,0:T(8,128)S(1)}, f32[2,1,128,128]{3,2,1,0:T(8,128)}, u32[]{:S(2)}) copy-start(f32[2,1,128,128]{3,2,1,0:T(8,128)} %refs_4_.1) | copy-start | bytes 393220
  21.9 32.4 %copy-start.1 = (bf16[4,256,256]{2,1,0:T(8,128)(2,1)S(1)}, bf16[4,256,256]{2,1,0:T(8,128)(2,1)}, u32[]{:S(2)}) copy-start(bf16[4,256,256]{2,1,0:T(8,128)(2,1)} %constant.15.clone.transform_ref) | copy-start | bytes 1572868

commit v3 on v2

--- a/solution.py
+++ b/solution.py
@@ -23,6 +23,8 @@
 HALO = REACH + HALF_WIN
 LANES = 128
 GROUPS = LANES // SPAN
+HALF_TILE = TILE * TILE // 2
+HALF_SPAN = (TILE // 2 + 2 * HALF_WIN) * SPAN
 AREA = float(WIN * WIN)
 LIMIT = 24 * 1024 * 1024
 
@@ -90,62 +92,113 @@
     return total
 
 
+def pack_tile(strip_piece, tile_col):
+    lane = iota((8, LANES), 1)
+    group = lane // SPAN
+    place = lane % SPAN
+    planes = []
+    for plane in range(2):
+        tile = None
+        for part in reversed(range(GROUPS)):
+            this = strip_piece((2 * part - tile_col) % (LANES // TILE), plane, part)
+            tile = this if tile is None else jnp.where(group == part, this, tile)
+        if tile_col == 0:
+            tile = jnp.where(place >= HALF_WIN, tile, 0.0)
+        if tile_col == LANES // TILE - 1:
+            tile = jnp.where(place < HALF_WIN + TILE, tile, 0.0)
+        planes.append(tile)
+    return jnp.concatenate(planes, axis=0).astype(BF16)
+
+
 def inner_kernel(
-    shift_ref, fraction_ref, table_ref, own_ref, exponent_ref, rolled_ref, mask_ref, exponent_out_ref
+    shift_ref, fraction_ref, table_ref, own_ref, exponent_ref,
+    packed_ref, near_ref, mask_ref, exponent_out_ref, step_ref, tap_ref, rolled,
 ):
     row_shift, col_shift, row_taps, col_taps = read_taps(shift_ref, fraction_ref, table_ref)
-    kept = own_ref.shape[2] - 2 * HALF_WIN
+    rows = own_ref.shape[2]
+    kept = rows - 2 * HALF_WIN
     opening = HALF_WIN - (TAPS // 2 - 1) + row_shift
+    tile_cols = LANES // TILE
     for plane in range(2):
         along = filter_rows(
             lambda first, size: own_ref[plane, 0, pl.ds(first, size), :], opening, kept, row_taps
         )
         total = filter_cols(along, col_shift, col_taps)
-        for turn in range(LANES // TILE):
-            rolled_ref[turn, plane] = pltpu.roll(total, HALF_WIN + TILE * turn, 1)
-    inner = TILE * TILE
-    at = iota((LANES, inner), 0)
-    pixel = iota((LANES, inner), 1)
+        for turn in range(tile_cols):
+            moved = pltpu.roll(total, HALF_WIN + TILE * turn, 1)
+            rolled[turn, plane] = moved
+            near_ref[0, turn, plane] = moved[0:HALO]
+            near_ref[1, turn, plane] = moved[kept - HALO : kept]
+    for tile_row in range(1, rows // TILE - 1):
+        first = (tile_row - 1) * TILE
+        for tile_col in range(tile_cols):
+            packed_ref[tile_row * tile_cols + tile_col] = pack_tile(
+                lambda turn, plane, part: rolled[
+                    turn, plane, pl.ds(first + part, 8, stride=GROUPS), :
+                ],
+                tile_col,
+            )
+    shape = mask_ref.shape
+    at = iota(shape, 0)
+    pixel = iota(shape, 1)
+    row_lag = at // SPAN - pixel // TILE
     col_lag = at % SPAN - pixel % TILE
+    row_ok = jnp.logical_and(row_lag >= 0, row_lag < WIN)
     col_ok = jnp.logical_and(col_lag >= 0, col_lag < WIN)
-    row_base = (at // SPAN) * 8 - pixel // TILE
-    for b in range(SPAN * SPAN // LANES):
-        row_lag = row_base + b
-        ok = jnp.logical_and(col_ok, jnp.logical_and(row_lag >= 0, row_lag < WIN))
-        mask_ref[b * LANES : (b + 1) * LANES, :] = jnp.where(ok, 1.0, 0.0).astype(BF16)
+    mask_ref[...] = jnp.where(jnp.logical_and(row_ok, col_ok), 1.0, 0.0).astype(BF16)
     exponent_out_ref[...] = exponent_ref[...]
+    step_ref[0:1, :] = jnp.full((1, LANES), row_shift, jnp.int32)
+    step_ref[1:2, :] = jnp.full((1, LANES), col_shift, jnp.int32)
+    for tap in range(TAPS):
+        tap_ref[tap : tap + 1, :] = jnp.full((1, LANES), row_taps[tap], F32)
+        tap_ref[TAPS + tap : TAPS + tap + 1, :] = jnp.full((1, LANES), col_taps[tap], F32)
 
 
 def inner_resample(shifts, fractions, own, exponents):
     rows = own.shape[2]
+    tiles = (rows // TILE) * (LANES // TILE)
     kept = rows - 2 * HALF_WIN
     smem = pl.BlockSpec(memory_space=SMEM)
     vmem = pl.BlockSpec(memory_space=VMEM)
     return pl.pallas_call(
         inner_kernel,
         out_shape=(
-            jax.ShapeDtypeStruct((LANES // TILE, 2, kept, LANES), F32),
-            jax.ShapeDtypeStruct((SPAN * SPAN, TILE * TILE), BF16),
+            jax.ShapeDtypeStruct((tiles, 2 * 8, LANES), BF16),
+            jax.ShapeDtypeStruct((2, LANES // TILE, 2, HALO, LANES), F32),
+            jax.ShapeDtypeStruct((HALF_SPAN, HALF_TILE), BF16),
             jax.ShapeDtypeStruct(exponents.shape, F32),
+            jax.ShapeDtypeStruct((2, LANES), jnp.int32),
+            jax.ShapeDtypeStruct((2 * TAPS, LANES), F32),
         ),
         in_specs=[smem] * 3 + [vmem] * 2,
-        out_specs=(vmem,) * 3,
+        out_specs=(vmem,) * 6,
+        scratch_shapes=[VMEM((LANES // TILE, 2, kept, LANES), F32)],
         compiler_params=pltpu.CompilerParams(vmem_limit_bytes=LIMIT),
         cost_estimate=pl.CostEstimate(flops=2000000, bytes_accessed=2000000, transcendentals=0),
         name="inner_resample",
     )(shifts, fractions, tap_table(), own, exponents)
 
 
+def az_block():
+    return lax.axis_index("az").astype(jnp.int32)
+
+
 def edge_kernel(
-    last_block, shift_ref, fraction_ref, table_ref, block_ref, own_ref, even_ref, odd_ref, rolled_ref,
-    out_ref, extended, edges,
+    last_block, step_ref, tap_ref, own_ref, even_ref, odd_ref, packed_in_ref, near_ref,
+    packed_ref, strip, extended,
 ):
     rows = own_ref.shape[2]
-    row_shift, col_shift, row_taps, col_taps = read_taps(shift_ref, fraction_ref, table_ref)
-    block = block_ref[0]
+    row_shift, col_shift = jnp.max(step_ref[0:1, :]), jnp.max(step_ref[1:2, :])
+    row_taps = [tap_ref[tap : tap + 1, :] for tap in range(TAPS)]
+    col_taps = [tap_ref[TAPS + tap : TAPS + tap + 1, :] for tap in range(TAPS)]
+    block = az_block()
     is_even = lax.rem(block, 2) == 0
     tile_cols = LANES // TILE
+    tile_rows = rows // TILE
     opening = HALO - HALF_WIN - (TAPS // 2 - 1) + row_shift
+    packed_ref[tile_cols : (tile_rows - 1) * tile_cols] = packed_in_ref[
+        tile_cols : (tile_rows - 1) * tile_cols
+    ]
     for side in range(2):
         row_at = iota((HALO, LANES), 0)
         if side == 0:
@@ -156,71 +209,52 @@
             from_even = even_ref[plane, 0]
             from_odd = odd_ref[plane, 0]
             if side == 0:
-                extended[0:HALO] = jnp.where(is_even, from_odd, from_even)
-                extended[HALO : 2 * HALO] = own_ref[plane, 0, 0:HALO]
+                extended[side, plane, 0:HALO] = jnp.where(is_even, from_odd, from_even)
+                extended[side, plane, HALO : 2 * HALO] = own_ref[plane, 0, 0:HALO]
             else:
-                extended[0:HALO] = own_ref[plane, 0, rows - HALO : rows]
-                extended[HALO : 2 * HALO] = jnp.where(is_even, from_even, from_odd)
+                extended[side, plane, 0:HALO] = own_ref[plane, 0, rows - HALO : rows]
+                extended[side, plane, HALO : 2 * HALO] = jnp.where(is_even, from_even, from_odd)
             along = filter_rows(
-                lambda first, size: extended[pl.ds(first, size), :], opening, HALO, row_taps
+                lambda first, size: extended[side, plane, pl.ds(first, size), :],
+                opening, HALO, row_taps,
             )
             total = jnp.where(inside, filter_cols(along, col_shift, col_taps), 0.0)
             for turn in range(tile_cols):
-                edges[turn, plane, side * HALO : (side + 1) * HALO] = pltpu.roll(
+                strip[side, turn, plane, side * HALO : (side + 1) * HALO] = pltpu.roll(
                     total, HALF_WIN + TILE * turn, 1
                 )
-
-    def piece(turn, plane, step):
-        last = rows // 8 + 2
-        if step < 2:
-            return edges[turn, plane, step * 8 : step * 8 + 8, :]
-        if step >= last - 2:
-            start = HALO + (step - last + 2) * 8
-            return edges[turn, plane, start : start + 8, :]
-        return rolled_ref[turn, plane, (step - 2) * 8 : (step - 1) * 8, :]
-
-    lane = iota((8, LANES), 1)
-    group = lane // SPAN
-    place = lane % SPAN
-    for tile_row in range(rows // TILE):
+                strip[side, turn, plane, (1 - side) * HALO : (2 - side) * HALO] = near_ref[
+                    side, turn, plane
+                ]
+        tile_row = side * (tile_rows - 1)
         for tile_col in range(tile_cols):
-            planes = []
-            for plane in range(2):
-                tile = None
-                for part in reversed(range(GROUPS)):
-                    this = piece((2 * part - tile_col) % tile_cols, plane, 2 * tile_row + part)
-                    tile = this if tile is None else jnp.where(group == part, this, tile)
-                if tile_col == 0:
-                    tile = jnp.where(place >= HALF_WIN, tile, 0.0)
-                if tile_col == tile_cols - 1:
-                    tile = jnp.where(place < HALF_WIN + TILE, tile, 0.0)
-                planes.append(tile)
-            both = jnp.concatenate(planes, axis=0)
-            out_ref[tile_row * tile_cols + tile_col] = both.astype(BF16)
-
-
-def edge_resample(last_block, shifts, fractions, block, own, even, odd, rolled):
-    rows = own.shape[2]
-    tiles = (rows // TILE) * (LANES // TILE)
-    smem = pl.BlockSpec(memory_space=SMEM)
+            packed_ref[tile_row * tile_cols + tile_col] = pack_tile(
+                lambda turn, plane, part: strip[
+                    side, turn, plane, pl.ds(part, 8, stride=GROUPS), :
+                ],
+                tile_col,
+            )
+
+
+def edge_resample(last_block, steps, taps, own, even, odd, packed, near):
     vmem = pl.BlockSpec(memory_space=VMEM)
     return pl.pallas_call(
         lambda *refs: edge_kernel(last_block, *refs),
-        out_shape=jax.ShapeDtypeStruct((tiles, 2 * 8, LANES), BF16),
-        in_specs=[smem] * 4 + [vmem] * 4,
+        out_shape=jax.ShapeDtypeStruct(packed.shape, packed.dtype),
+        in_specs=[vmem] * 7,
         out_specs=vmem,
         scratch_shapes=[
-            VMEM((2 * HALO, LANES), F32),
-            VMEM((LANES // TILE, 2, 2 * HALO, LANES), F32),
+            VMEM((2, LANES // TILE, 2, 2 * HALO, LANES), F32),
+            VMEM((2, 2, 2 * HALO, LANES), F32),
         ],
         compiler_params=pltpu.CompilerParams(vmem_limit_bytes=LIMIT),
         name="edge_resample",
-    )(shifts, fractions, tap_table(), block, own, even, odd, rolled)
+    )(steps, taps, own, even, odd, packed, near)
 
 
 def link_kernel(
     tile_ref, exponent_ref, transform_ref, mask, out_ref,
-    loose, planes, pixels, power, weights, vector,
+    loose, planes, pixels, power, vector,
 ):
     dates = tile_ref.shape[0]
     count = 2 * dates
@@ -239,39 +273,38 @@
         high, low = split(real * real + imag * imag)
         power[0:dates, here] = high
         power[dates:count, here] = low
-    sums = dot(power[...], mask[...])
+    starts = [half * (SPAN * TILE // 2) for half in range(2)]
+    keep = mask[...]
+    sums = jnp.concatenate([dot(power[:, first : first + HALF_SPAN], keep) for first in starts], axis=1)
     scaling = lax.rsqrt((sums[:dates] + sums[dates:]) / AREA + EPS)
     vector[0] = jnp.ones((dates, inner), F32)
     vector[1] = jnp.zeros((dates, inner), F32)
 
     def iterate(_, carry):
-        real, imag = vector[0], vector[1]
-        scaled_real, scaled_imag = scaling * real, scaling * imag
-        rh, rl = split(scaled_real)
-        ih, il = split(scaled_imag)
-        weights[0:dates, 0:inner] = rh
-        weights[0:dates, inner:] = ih
-        weights[dates:count, 0:inner] = ih
-        weights[dates:count, inner:] = -rh
-        weights[count : count + dates, 0:inner] = rl
-        weights[count : count + dates, inner:] = il
-        weights[count + dates :, 0:inner] = il
-        weights[count + dates :, inner:] = -rl
-        total = jnp.zeros((count, 2 * inner), F32)
-        step = 256
-        for first in range(0, SPAN * SPAN, step):
-            here = slice(first, first + step)
-            inner_products = dot(pixels[here, :], weights[...])
-            keep = mask[here, :].astype(F32)
-            high, low = split(inner_products * jnp.concatenate([keep, keep], axis=1))
-            total = total + dot(planes[:, here], high) + dot(planes[:, here], low)
-        factor = scaling / AREA
-        new_real = factor * (total[:dates, :inner] - total[dates:, inner:]) + DAMP * real
-        new_imag = factor * (total[:dates, inner:] + total[dates:, :inner]) + DAMP * imag
-        square = jnp.sum(new_real * new_real + new_imag * new_imag, axis=0, keepdims=True)
-        inverse = lax.rsqrt(square / dates + EPS)
-        vector[0] = new_real * inverse
-        vector[1] = new_imag * inverse
+        for half in range(2):
+            cols = slice(half * HALF_TILE, (half + 1) * HALF_TILE)
+            real, imag = vector[0, :, cols], vector[1, :, cols]
+            scale = scaling[:, cols]
+            rh, rl = split(scale * real)
+            ih, il = split(scale * imag)
+            top = [jnp.concatenate(pair, axis=1) for pair in ((rh, ih), (ih, -rh), (rl, il), (il, -rl))]
+            weights = jnp.concatenate(top, axis=0)
+            total = jnp.zeros((count, 2 * HALF_TILE), F32)
+            step = 256
+            for first in range(0, HALF_SPAN, step):
+                here = slice(starts[half] + first, starts[half] + first + step)
+                near = mask[first : first + step, :].astype(F32)
+                products = dot(pixels[here, :], weights)
+                kept = (products * jnp.concatenate([near, near], axis=1)).astype(BF16)
+                total = total + dot(planes[:, here], kept)
+            factor = scale / AREA
+            left, right = slice(0, HALF_TILE), slice(HALF_TILE, 2 * HALF_TILE)
+            new_real = factor * (total[:dates, left] - total[dates:, right]) + DAMP * real
+            new_imag = factor * (total[:dates, right] + total[dates:, left]) + DAMP * imag
+            square = jnp.sum(new_real * new_real + new_imag * new_imag, axis=0, keepdims=True)
+            inverse = lax.rsqrt(square / dates + EPS)
+            vector[0, :, cols] = new_real * inverse
+            vector[1, :, cols] = new_imag * inverse
         return carry
 
     lax.fori_loop(0, ITERS, iterate, 0)
@@ -311,7 +344,6 @@
             VMEM((2 * dates, outer), BF16),
             VMEM((outer, 4 * dates), BF16),
             VMEM((2 * dates, outer), BF16),
-            VMEM((4 * dates, 2 * inner), BF16),
             VMEM((2, dates, inner), F32),
         ],
         compiler_params=pltpu.CompilerParams(vmem_limit_bytes=LIMIT),
@@ -363,7 +395,7 @@
 def local(images, shifts, fractions, exponents):
     rows = images.shape[2]
     blocks = lax.axis_size("az")
-    block = lax.axis_index("az").astype(jnp.int32)
+    block = az_block()
     first = lax.slice_in_dim(images, 0, HALO, axis=2)
     last = lax.slice_in_dim(images, rows - HALO, rows, axis=2)
     is_even = lax.rem(block, 2) == 0
@@ -371,12 +403,10 @@
     to_even = jnp.where(is_even, last, first)
     odd = lax.ppermute(to_odd, "az", both_ways(range(1, blocks - 1, 2)))
     even = lax.ppermute(to_even, "az", both_ways(range(0, blocks - 1, 2)))
-    rolled, mask, exponent_row = inner_resample(
+    packed, near, mask, exponent_row, steps, tap_rows = inner_resample(
         shifts, fractions, images, exponents.reshape(1, exponents.shape[0])
     )
-    packed = edge_resample(
-        blocks - 1, shifts, fractions, block.reshape(1), images, even, odd, rolled
-    )
+    packed = edge_resample(blocks - 1, steps, tap_rows, images, even, odd, packed, near)
     tile = lax.all_to_all(packed, "date", split_axis=0, concat_axis=0, tiled=True)
     filtered = link(tile, exponent_row, mask)
     filtered = filtered.reshape(filtered.shape[0], -1, LANES)

time: 78.3 us -> 77.1 us (0.985)
  Pallas kernels: 7.8 us -> 6.51 us
  transfers between devices with their start and end apart: 2 -> 2, of which waited for: 0 -> 1; matrix products, arithmetic and copies ran while one was open for 0% -> 0% of each run, Pallas kernels for 2% -> 2%
where the time goes in v3:
time: 77.1 us; the launch traced here: 76.8 us
  blocking collectives  51 us (66%)
  starting transfers between devices  17.4 us (23%)
  Pallas kernels  6.51 us (8%)
  local copies, waits for them, and re-layouts  0.96 us (1%)
    all_to_all x1, blocking collectives, local(): lax.all_to_all(packed, 'date', split_axis=0, concat_axis=0, tiled=True)  32.5 us
    all_to_all x1, blocking collectives, local(): lax.all_to_all(filtered, 'date', split_axis=0, concat_axis=0, tiled=True)  18.6 us
    ppermute x1, starting transfers between devices, local(): odd = lax.ppermute(to_odd, 'az', both_ways(range(1, blocks - 1, 2)))  15.3 us
    pallas_call x1, Pallas kernels, link(): pl.pallas_call(link_kernel, out_shape=jax.ShapeDtypeStruct((dates, 2 * in...  3.61 us
    ppermute x1, starting transfers between devices, local(): even = lax.ppermute(to_even, 'az', both_ways(range(0, blocks - 1, 2)))  2.05 us
  transfers between devices with their start and end apart: 2, of which 1 were waited for; matrix products, arithmetic and copies ran while one was open for 0% of the time, Pallas kernels for 2%

profile of v3, /device:TPU:7, one launch (start us, length us, event | category | flops | bytes accessed | tf_op | source)
XLA Modules:
  0.0 76.8 jit_solution(12004671676682961956)
XLA Ops:
  0.0 0.0 copy-start.3
  0.0 0.8 slice_select_fusion
  0.8 15.3 %collective-permute-start.1 = (f32[2,1,16,128]{3,2,1,0:T(8,128)S(1)}, f32[2,1,16,128]{3,2,1,0:T(8,128)S(1)}, u32[]{:S(2)}, u32[]{:S(2)}) collective-permute-start(f32[2,1,16,128]{3,2,1,0:T(8,128)S(1)} %get-tuple-element.17), channel_id=1, source_target_pairs={{1,2},{3,4},{5,6},{2,1},{4,3},{6,5},{9,10},{11,12},{13,14},{10,9},... | collective-permute-start | bytes 49160 | tf_op jit(solution)/shard_map/ppermute | solution.py:404
  16.1 0.0 copy-start.4
  16.1 0.0 copy-start.5
  16.1 0.0 copy-start.6
  16.1 2.1 %collective-permute-start = (f32[2,1,16,128]{3,2,1,0:T(8,128)S(1)}, f32[2,1,16,128]{3,2,1,0:T(8,128)S(1)}, u32[]{:S(2)}, u32[]{:S(2)}) collective-permute-start(f32[2,1,16,128]{3,2,1,0:T(8,128)S(1)} %get-tuple-element.18), channel_id=1, source_target_pairs={{0,1},{2,3},{4,5},{6,7},{1,0},{3,2},{5,4},{7,6},{8,9},{10,11},{12,... | collective-permute-start | bytes 49160 | tf_op jit(solution)/shard_map/ppermute | solution.py:405
  18.2 0.0 copy-done.3
  18.2 0.0 copy-done.4
  18.2 0.0 copy-done.5
  18.2 0.0 copy-done.6
  18.2 0.0 copy-start
  18.3 0.9 %copy-done = f32[2,1,128,128]{3,2,1,0:T(8,128)S(1)} copy-done((f32[2,1,128,128]{3,2,1,0:T(8,128)S(1)}, f32[2,1,128,128]{3,2,1,0:T(8,128)}, u32[]{:S(2)}) %copy-start) | copy-done | bytes 131096
  19.2 0.0 copy-start.1
  19.2 1.5 %inner_resample.1 = (bf16[64,16,128]{2,1,0:T(8,128)(2,1)S(1)}, f32[2,8,2,16,128]{4,3,2,1,0:T(8,128)S(1)}, bf16[768,128]{1,0:T(8,128)(2,1)S(1)}, f32[1,64]{1,0:T(...) custom-call(s32[1,2]{1,0:T(1,128)S(1)} %copy-done.4, s32[1,2]{1,0:T(1,128)S(1)} %copy-done.5, ...), custom_call_target="tpu_custom_call" | custom-call | flops 2000000 | bytes 2000000 | tf_op jit(solution)/shard_map/inner_resample/pallas_call | solution.py:163
  20.7 0.0 collective-permute-done.1.refs_4_
  20.7 0.1 collective-permute-done.refs_3_
  20.8 0.0 copy-done.1
  20.8 0.5 edge_resample.1
  21.2 32.5 %all_to_all.10.tile_ref = bf16[64,16,128]{2,1,0:T(8,128)(2,1)S(1)} all-to-all(bf16[64,16,128]{2,1,0:T(8,128)(2,1)S(1)} %edge_resample.1), channel_id=1, replica_groups=mesh['date'=64,'az'=8] {'date'}, dimensions={0} | all-to-all | bytes 524288 | tf_op jit(solution)/shard_map/all_to_all | solution.py:410
  53.7 0.0 copy-done.2
  53.7 3.6 %link.1 = bf16[64,512]{1,0:T(8,128)(2,1)S(1)} custom-call(bf16[64,16,128]{2,1,0:T(8,128)(2,1)S(1)} %all_to_all.10.tile_ref, f32[1,64]{1,0:T(1,128)S(1)} %get-tuple-element.15.exponent_ref, bf16[4,256,256]{2,1,0:T(8,128)(2,1)S(1)} %copy-done.2, bf16[768,128]{1,0:T(8,128)(2,1)S(1)} %get-tuple-element.16.mask), custom_call_target="tpu_custom_call" | custom-call | tf_op jit(solution)/shard_map/link/pallas_call | solution.py:337
  57.3 18.6 %all_to_all.11 = bf16[64,4,128]{2,1,0:T(4,128)(2,1)S(1)} all-to-all(bf16[64,4,128]{2,1,0:T(4,128)(2,1)S(1)} %reshape.10), channel_id=1, replica_groups=mesh['date'=64,'az'=8] {'date'}, dimensions={0} | all-to-all | bytes 131072 | tf_op jit(solution)/shard_map/all_to_all | solution.py:413
  75.9 0.9 %unpack.1 = f32[2,1,128,128]{3,2,1,0:T(8,128)} custom-call(bf16[64,512]{1,0:T(8,128)(2,1)S(1)} %bitcast.5), custom_call_target="tpu_custom_call" | custom-call | tf_op jit(solution)/shard_map/unpack/pallas_call | solution.py:381
  (3 shorter events, 0.0 us)
Async XLA Ops:
  0.0 18.2 %copy-start.3 = (f32[16,8]{1,0:T(8,128)S(1)}, f32[16,8]{1,0:T(8,128)}, u32[]{:S(2)}) copy-start(f32[16,8]{1,0:T(8,128)} %constant.14.clone.table_ref) | copy-start | bytes 1540
  0.8 19.9 %collective-permute-start.1 = (f32[2,1,16,128]{3,2,1,0:T(8,128)S(1)}, f32[2,1,16,128]{3,2,1,0:T(8,128)S(1)}, u32[]{:S(2)}, u32[]{:S(2)}) collective-permute-start(f32[2,1,16,128]{3,2,1,0:T(8,128)S(1)} %get-tuple-element.17), channel_id=1, source_target_pairs={{1,2},{3,4},{5,6},{2,1},{4,3},{6,5},{9,10},{11,12},{13,14},{10,9},... | collective-permute-start | bytes 49160 | tf_op jit(solution)/shard_map/ppermute | solution.py:404
  16.1 2.1 %copy-start.4 = (s32[1,2]{1,0:T(1,128)S(1)}, s32[1,2]{1,0:T(1,128)}, u32[]{:S(2)}) copy-start(s32[1,2]{1,0:T(1,128)} %shift_ref.1) | copy-start | bytes 28
  16.1 2.1 %copy-start.5 = (s32[1,2]{1,0:T(1,128)S(1)}, s32[1,2]{1,0:T(1,128)}, u32[]{:S(2)}) copy-start(s32[1,2]{1,0:T(1,128)} %fraction_ref.1) | copy-start | bytes 28
  16.1 2.1 %copy-start.6 = (f32[64]{0:T(128)S(1)}, f32[64]{0:T(128)}, u32[]{:S(2)}) copy-start(f32[64]{0:T(128)} %param.9) | copy-start | bytes 772
  16.1 4.6 %collective-permute-start = (f32[2,1,16,128]{3,2,1,0:T(8,128)S(1)}, f32[2,1,16,128]{3,2,1,0:T(8,128)S(1)}, u32[]{:S(2)}, u32[]{:S(2)}) collective-permute-start(f32[2,1,16,128]{3,2,1,0:T(8,128)S(1)} %get-tuple-element.18), channel_id=1, source_target_pairs={{0,1},{2,3},{4,5},{6,7},{1,0},{3,2},{5,4},{7,6},{8,9},{10,11},{12,... | collective-permute-start | bytes 49160 | tf_op jit(solution)/shard_map/ppermute | solution.py:405
  18.2 0.9 %copy-start = (f32[2,1,128,128]{3,2,1,0:T(8,128)S(1)}, f32[2,1,128,128]{3,2,1,0:T(8,128)}, u32[]{:S(2)}) copy-start(f32[2,1,128,128]{3,2,1,0:T(8,128)} %refs_2_.1) | copy-start | bytes 393220
  19.2 1.6 %copy-start.1 = (f32[2,1,128,128]{3,2,1,0:T(8,128)S(1)}, f32[2,1,128,128]{3,2,1,0:T(8,128)}, u32[]{:S(2)}) copy-start(f32[2,1,128,128]{3,2,1,0:T(8,128)} %refs_2_.1) | copy-start | bytes 393220
  20.8 32.9 %copy-start.2 = (bf16[4,256,256]{2,1,0:T(8,128)(2,1)S(1)}, bf16[4,256,256]{2,1,0:T(8,128)(2,1)}, u32[]{:S(2)}) copy-start(bf16[4,256,256]{2,1,0:T(8,128)(2,1)} %constant.15.clone.transform_ref) | copy-start | bytes 1572868

commit v4 on v3

--- a/solution.py
+++ b/solution.py
@@ -184,7 +184,8 @@
 
 
 def edge_kernel(
-    last_block, step_ref, tap_ref, own_ref, even_ref, odd_ref, packed_in_ref, near_ref,
+    below, last_block, step_ref, tap_ref, own_ref, one_ref, two_ref, three_ref, down_ref,
+    packed_in_ref, near_ref,
     packed_ref, strip, extended,
 ):
     rows = own_ref.shape[2]
@@ -192,7 +193,10 @@
     row_taps = [tap_ref[tap : tap + 1, :] for tap in range(TAPS)]
     col_taps = [tap_ref[TAPS + tap : TAPS + tap + 1, :] for tap in range(TAPS)]
     block = az_block()
-    is_even = lax.rem(block, 2) == 0
+    chosen = [
+        [jnp.bitwise_and(jnp.right_shift(jnp.int32(bits << shift), block), 1) == 1 for bits in below]
+        for shift in (1, 0)
+    ]
     tile_cols = LANES // TILE
     tile_rows = rows // TILE
     opening = HALO - HALF_WIN - (TAPS // 2 - 1) + row_shift
@@ -206,14 +210,15 @@
         else:
             inside = jnp.logical_or(block < last_block, row_at < HALF_WIN)
         for plane in range(2):
-            from_even = even_ref[plane, 0]
-            from_odd = odd_ref[plane, 0]
+            from_near = jnp.zeros((HALO, LANES), F32)
+            for take, near_by in zip(chosen[side], (one_ref, two_ref, three_ref)):
+                from_near = jnp.where(take, near_by[plane, 0], from_near)
             if side == 0:
-                extended[side, plane, 0:HALO] = jnp.where(is_even, from_odd, from_even)
+                extended[side, plane, 0:HALO] = from_near
                 extended[side, plane, HALO : 2 * HALO] = own_ref[plane, 0, 0:HALO]
             else:
                 extended[side, plane, 0:HALO] = own_ref[plane, 0, rows - HALO : rows]
-                extended[side, plane, HALO : 2 * HALO] = jnp.where(is_even, from_even, from_odd)
+                extended[side, plane, HALO : 2 * HALO] = from_near + down_ref[plane, 0]
             along = filter_rows(
                 lambda first, size: extended[side, plane, pl.ds(first, size), :],
                 opening, HALO, row_taps,
@@ -236,12 +241,12 @@
             )
 
 
-def edge_resample(last_block, steps, taps, own, even, odd, packed, near):
+def edge_resample(below, last_block, steps, taps, own, moved, packed, near):
     vmem = pl.BlockSpec(memory_space=VMEM)
     return pl.pallas_call(
-        lambda *refs: edge_kernel(last_block, *refs),
+        lambda *refs: edge_kernel(below, last_block, *refs),
         out_shape=jax.ShapeDtypeStruct(packed.shape, packed.dtype),
-        in_specs=[vmem] * 7,
+        in_specs=[vmem] * 9,
         out_specs=vmem,
         scratch_shapes=[
             VMEM((2, LANES // TILE, 2, 2 * HALO, LANES), F32),
@@ -249,7 +254,7 @@
         ],
         compiler_params=pltpu.CompilerParams(vmem_limit_bytes=LIMIT),
         name="edge_resample",
-    )(steps, taps, own, even, odd, packed, near)
+    )(steps, taps, own, *moved, packed, near)
 
 
 def link_kernel(
@@ -388,25 +393,51 @@
     )(tiles)
 
 
-def both_ways(boundaries):
-    return [(k, k + 1) for k in boundaries] + [(k + 1, k) for k in boundaries]
+def both_ways(boundaries, dates, blocks):
+    pairs = [(k, k + 1) for k in boundaries] + [(k + 1, k) for k in boundaries]
+    return [(d * blocks + i, d * blocks + j) for d in dates for i, j in pairs]
+
+
+def after(value, *earlier):
+    return lax.optimization_barrier((value, *earlier))[0]
 
 
 def local(images, shifts, fractions, exponents):
     rows = images.shape[2]
     blocks = lax.axis_size("az")
+    dates = lax.axis_size("date")
+    middle = blocks // 2 - 1
     block = az_block()
     first = lax.slice_in_dim(images, 0, HALO, axis=2)
     last = lax.slice_in_dim(images, rows - HALO, rows, axis=2)
-    is_even = lax.rem(block, 2) == 0
-    to_odd = jnp.where(is_even, first, last)
-    to_even = jnp.where(is_even, last, first)
-    odd = lax.ppermute(to_odd, "az", both_ways(range(1, blocks - 1, 2)))
-    even = lax.ppermute(to_even, "az", both_ways(range(0, blocks - 1, 2)))
+    late = range(dates // 2, dates)
+
+    def move(value, pairs):
+        return lax.ppermute(value, ("date", "az"), pairs)
+
+    def edge(boundaries):
+        lower = sum(1 << k for k in boundaries)
+        sends_last = jnp.bitwise_and(jnp.right_shift(jnp.int32(lower), block), 1) == 1
+        return jnp.where(sends_last, last, first)
+
+    sets = ([k for k in range(blocks - 1) if k != middle and (k + (k > middle)) % 2 == 0],
+            [k for k in range(blocks - 1) if k == middle or (k < middle and k % 2 == 1)],
+            [k for k in range(middle + 1, blocks - 1) if (k + 1) % 2 == 1])
+    half = dates // 2
+    relay = move(first, [(d * blocks + middle + 1, (d - half) * blocks) for d in late])
+    down = move(relay, [((d - half) * blocks, d * blocks + middle) for d in late])
+    one = move(after(edge(sets[0]), relay), both_ways(sets[0], range(dates), blocks))
+    pairs = both_ways(sets[1], range(dates), blocks)
+    skipped = {(d * blocks + middle + 1, d * blocks + middle) for d in late}
+    two = move(after(edge(sets[1]), relay), [p for p in pairs if p not in skipped])
+    three = move(after(edge(sets[2]), relay), both_ways(sets[2], range(dates), blocks))
+    below = [sum(1 << k for k in chosen) for chosen in sets]
     packed, near, mask, exponent_row, steps, tap_rows = inner_resample(
         shifts, fractions, images, exponents.reshape(1, exponents.shape[0])
     )
-    packed = edge_resample(blocks - 1, steps, tap_rows, images, even, odd, packed, near)
+    packed = edge_resample(
+        below, blocks - 1, steps, tap_rows, images, (one, two, three, down), packed, near
+    )
     tile = lax.all_to_all(packed, "date", split_axis=0, concat_axis=0, tiled=True)
     filtered = link(tile, exponent_row, mask)
     filtered = filtered.reshape(filtered.shape[0], -1, LANES)

time: 77.1 us -> 84.7 us (1.099)
  blocking collectives: 51 us -> 58 us
    all_to_all x1, blocking collectives: 32.5 us -> 39.4 us  [local(): lax.all_to_all(packed, 'date', split_axis=0, concat_axis=0, tiled=True)]
    ppermute x2 -> x5, starting transfers between devices: 17.4 us -> 18.1 us  [move(): return lax.ppermute(value, ('date', 'az'), pairs)]
  transfers between devices with their start and end apart: 2 -> 5, of which waited for: 1 -> 0; matrix products, arithmetic and copies ran while one was open for 0% -> 0% of each run, Pallas kernels for 2% -> 2%
where the time goes in v4:
time: 84.7 us; the launch traced here: 84.4 us
  blocking collectives  58 us (68%)
  starting transfers between devices  18.1 us (21%)
  Pallas kernels  6.51 us (8%)
    all_to_all x1, blocking collectives, local(): lax.all_to_all(packed, 'date', split_axis=0, concat_axis=0, tiled=True)  39.4 us
    all_to_all x1, blocking collectives, local(): lax.all_to_all(filtered, 'date', split_axis=0, concat_axis=0, tiled=True)  18.6 us
    ppermute x5, starting transfers between devices, move(): return lax.ppermute(value, ('date', 'az'), pairs)  18.1 us
    pallas_call x1, Pallas kernels, link(): pl.pallas_call(link_kernel, out_shape=jax.ShapeDtypeStruct((dates, 2 * in...  3.61 us
  transfers between devices with their start and end apart: 5, of which 0 were waited for; matrix products, arithmetic and copies ran while one was open for 0% of the time, Pallas kernels for 2%

profile of v4, /device:TPU:7, one launch (start us, length us, event | category | flops | bytes accessed | tf_op | source)
XLA Modules:
  0.0 84.4 jit_solution(2331234773023556907)
XLA Ops:
  0.0 0.8 slice_select_fusion
  0.8 0.7 collective-permute-start
  1.5 0.0 collective-permute-done
  1.5 0.0 copy-start.3
  1.5 0.0 copy-start.4
  1.5 0.0 copy-start.5
  1.5 2.6 %collective-permute-start.1 = (f32[2,1,16,128]{3,2,1,0:T(8,128)S(1)}, f32[2,1,16,128]{3,2,1,0:T(8,128)S(1)}, u32[]{:S(2)}, u32[]{:S(2)}) collective-permute-start(f32[2,1,16,128]{3,2,1,0:T(8,128)S(1)} %get-tuple-element.16), channel_id=1, source_target_pairs={{0,1},{2,3},{5,6},{1,0},{3,2},{6,5},{8,9},{10,11},{13,14},{9,8},{1... | collective-permute-start | bytes 49160 | tf_op jit(solution)/shard_map/ppermute | solution.py:416
  4.1 13.6 %collective-permute-start.2 = (f32[2,1,16,128]{3,2,1,0:T(8,128)S(1)}, f32[2,1,16,128]{3,2,1,0:T(8,128)S(1)}, u32[]{:S(2)}, u32[]{:S(2)}) collective-permute-start(f32[2,1,16,128]{3,2,1,0:T(8,128)S(1)} %get-tuple-element.17), channel_id=1, source_target_pairs={{1,2},{3,4},{2,1},{4,3},{9,10},{11,12},{10,9},{12,11},{17,18},{19,... | collective-permute-start | bytes 49160 | tf_op jit(solution)/shard_map/ppermute | solution.py:416
  17.7 0.7 collective-permute-start.3
  18.3 0.7 collective-permute-start.4
  19.0 0.0 copy-done
  19.1 0.0 copy-start.2
  19.1 0.7 copy-done.2
  19.8 1.5 %inner_resample.1 = (bf16[64,16,128]{2,1,0:T(8,128)(2,1)S(1)}, f32[2,8,2,16,128]{4,3,2,1,0:T(8,128)S(1)}, bf16[768,128]{1,0:T(8,128)(2,1)S(1)}, f32[1,64]{1,0:T(...) custom-call(s32[1,2]{1,0:T(1,128)S(1)} %copy-done.3, s32[1,2]{1,0:T(1,128)S(1)} %copy-done.4, ...), custom_call_target="tpu_custom_call" | custom-call | flops 2000000 | bytes 2000000 | tf_op jit(solution)/shard_map/inner_resample/pallas_call | solution.py:163
  21.3 0.0 collective-permute-done.1.refs_3_
  21.3 0.0 collective-permute-done.2.refs_4_
  21.3 0.0 collective-permute-done.3.refs_5_
  21.3 0.0 collective-permute-done.4.refs_6_
  21.3 0.0 copy-start.1
  21.3 0.5 edge_resample.1
  21.8 39.4 %all_to_all.10.tile_ref = bf16[64,16,128]{2,1,0:T(8,128)(2,1)S(1)} all-to-all(bf16[64,16,128]{2,1,0:T(8,128)(2,1)S(1)} %edge_resample.1), channel_id=1, replica_groups=mesh['date'=64,'az'=8] {'date'}, dimensions={0} | all-to-all | bytes 524288 | tf_op jit(solution)/shard_map/all_to_all | solution.py:441
  61.3 3.6 %link.1 = bf16[64,512]{1,0:T(8,128)(2,1)S(1)} custom-call(bf16[64,16,128]{2,1,0:T(8,128)(2,1)S(1)} %all_to_all.10.tile_ref, f32[1,64]{1,0:T(1,128)S(1)} %get-tuple-element.21.exponent_ref, bf16[4,256,256]{2,1,0:T(8,128)(2,1)S(1)} %copy-done.1, bf16[768,128]{1,0:T(8,128)(2,1)S(1)} %get-tuple-element.22.mask), custom_call_target="tpu_custom_call" | custom-call | tf_op jit(solution)/shard_map/link/pallas_call | solution.py:342
  64.9 18.6 %all_to_all.11 = bf16[64,4,128]{2,1,0:T(4,128)(2,1)S(1)} all-to-all(bf16[64,4,128]{2,1,0:T(4,128)(2,1)S(1)} %reshape.10), channel_id=1, replica_groups=mesh['date'=64,'az'=8] {'date'}, dimensions={0} | all-to-all | bytes 131072 | tf_op jit(solution)/shard_map/all_to_all | solution.py:444
  83.5 0.9 %unpack.1 = f32[2,1,128,128]{3,2,1,0:T(8,128)} custom-call(bf16[64,512]{1,0:T(8,128)(2,1)S(1)} %bitcast.5), custom_call_target="tpu_custom_call" | custom-call | tf_op jit(solution)/shard_map/unpack/pallas_call | solution.py:386
  (7 shorter events, 0.0 us)
Async XLA Ops:
  0.0 19.0 %copy-start = (f32[2,1,128,128]{3,2,1,0:T(8,128)S(1)}, f32[2,1,128,128]{3,2,1,0:T(8,128)}, u32[]{:S(2)}) copy-start(f32[2,1,128,128]{3,2,1,0:T(8,128)} %refs_2_.1) | copy-start | bytes 393220
  0.8 0.7 collective-permute-start
  1.5 17.6 %copy-start.3 = (s32[1,2]{1,0:T(1,128)S(1)}, s32[1,2]{1,0:T(1,128)}, u32[]{:S(2)}) copy-start(s32[1,2]{1,0:T(1,128)} %shift_ref.1) | copy-start | bytes 28
  1.5 17.6 %copy-start.4 = (s32[1,2]{1,0:T(1,128)S(1)}, s32[1,2]{1,0:T(1,128)}, u32[]{:S(2)}) copy-start(s32[1,2]{1,0:T(1,128)} %fraction_ref.1) | copy-start | bytes 28
  1.5 17.6 %copy-start.5 = (f32[64]{0:T(128)S(1)}, f32[64]{0:T(128)}, u32[]{:S(2)}) copy-start(f32[64]{0:T(128)} %param.9) | copy-start | bytes 772
  1.5 19.8 %collective-permute-start.1 = (f32[2,1,16,128]{3,2,1,0:T(8,128)S(1)}, f32[2,1,16,128]{3,2,1,0:T(8,128)S(1)}, u32[]{:S(2)}, u32[]{:S(2)}) collective-permute-start(f32[2,1,16,128]{3,2,1,0:T(8,128)S(1)} %get-tuple-element.16), channel_id=1, source_target_pairs={{0,1},{2,3},{5,6},{1,0},{3,2},{6,5},{8,9},{10,11},{13,14},{9,8},{1... | collective-permute-start | bytes 49160 | tf_op jit(solution)/shard_map/ppermute | solution.py:416
  4.1 17.2 %collective-permute-start.2 = (f32[2,1,16,128]{3,2,1,0:T(8,128)S(1)}, f32[2,1,16,128]{3,2,1,0:T(8,128)S(1)}, u32[]{:S(2)}, u32[]{:S(2)}) collective-permute-start(f32[2,1,16,128]{3,2,1,0:T(8,128)S(1)} %get-tuple-element.17), channel_id=1, source_target_pairs={{1,2},{3,4},{2,1},{4,3},{9,10},{11,12},{10,9},{12,11},{17,18},{19,... | collective-permute-start | bytes 49160 | tf_op jit(solution)/shard_map/ppermute | solution.py:416
  17.7 3.6 %collective-permute-start.3 = (f32[2,1,16,128]{3,2,1,0:T(8,128)S(1)}, f32[2,1,16,128]{3,2,1,0:T(8,128)S(1)}, u32[]{:S(2)}, u32[]{:S(2)}) collective-permute-start(f32[2,1,16,128]{3,2,1,0:T(8,128)S(1)} %get-tuple-element.18), channel_id=1, source_target_pairs={{4,5},{6,7},{5,4},{7,6},{12,13},{14,15},{13,12},{15,14},{20,21},{2... | collective-permute-start | bytes 49160 | tf_op jit(solution)/shard_map/ppermute | solution.py:416
  18.3 3.0 %collective-permute-start.4 = (f32[2,1,16,128]{3,2,1,0:T(8,128)S(1)}, f32[2,1,16,128]{3,2,1,0:T(8,128)S(1)}, u32[]{:S(2)}, u32[]{:S(2)}) collective-permute-start(f32[2,1,16,128]{3,2,1,0:T(8,128)S(1)} %collective-permute-done), channel_id=1, source_target_pairs={{0,259},{8,267},{16,275},{24,283},{32,291},{40,299},{48,307},{56,3... | collective-permute-start | bytes 49160 | tf_op jit(solution)/shard_map/ppermute | solution.py:416
  19.1 0.7 copy-start.2
  21.3 39.9 %copy-start.1 = (bf16[4,256,256]{2,1,0:T(8,128)(2,1)S(1)}, bf16[4,256,256]{2,1,0:T(8,128)(2,1)}, u32[]{:S(2)}) copy-start(bf16[4,256,256]{2,1,0:T(8,128)(2,1)} %constant.17.clone.transform_ref) | copy-start | bytes 1572868

commit v5 on v4

--- a/solution.py
+++ b/solution.py
@@ -29,7 +29,6 @@
 LIMIT = 24 * 1024 * 1024
 
 VMEM = pltpu.VMEM
-SMEM = pltpu.SMEM
 F32 = jnp.float32
 BF16 = jnp.bfloat16
 
@@ -67,10 +66,22 @@
     return jnp.dot(a, b, preferred_element_type=F32)
 
 
-def read_taps(shift_ref, fraction_ref, table_ref):
-    row_taps = [table_ref[fraction_ref[0, 0], tap] for tap in range(TAPS)]
-    col_taps = [table_ref[fraction_ref[0, 1], tap] for tap in range(TAPS)]
-    return shift_ref[0, 0], shift_ref[0, 1], row_taps, col_taps
+def pick(values, bits):
+    if not bits:
+        return values[0]
+    return jnp.where(bits[0], pick(values[1::2], bits[1:]), pick(values[0::2], bits[1:]))
+
+
+def lane_value(ref, lane):
+    row = ref[...]
+    return jnp.max(jnp.where(iota(row.shape, 1) == lane, row, -TAPS * FRAC))
+
+
+def taps_of(ref, lane):
+    table = tap_table()
+    fraction = jnp.broadcast_to(ref[:, lane : lane + 1], (1, LANES))
+    bits = [jnp.bitwise_and(jnp.right_shift(fraction, k), 1) == 1 for k in range(4)]
+    return [pick([float(value) for value in table[:, tap]], bits) for tap in range(TAPS)]
 
 
 def filter_rows(source, opening, kept, taps):
@@ -111,10 +122,11 @@
 
 
 def inner_kernel(
-    shift_ref, fraction_ref, table_ref, own_ref, exponent_ref,
+    shift_ref, fraction_ref, own_ref, exponent_ref,
     packed_ref, near_ref, mask_ref, exponent_out_ref, step_ref, tap_ref, rolled,
 ):
-    row_shift, col_shift, row_taps, col_taps = read_taps(shift_ref, fraction_ref, table_ref)
+    row_shift, col_shift = lane_value(shift_ref, 0), lane_value(shift_ref, 1)
+    row_taps, col_taps = (taps_of(fraction_ref, lane) for lane in range(2))
     rows = own_ref.shape[2]
     kept = rows - 2 * HALF_WIN
     opening = HALF_WIN - (TAPS // 2 - 1) + row_shift
@@ -150,15 +162,14 @@
     step_ref[0:1, :] = jnp.full((1, LANES), row_shift, jnp.int32)
     step_ref[1:2, :] = jnp.full((1, LANES), col_shift, jnp.int32)
     for tap in range(TAPS):
-        tap_ref[tap : tap + 1, :] = jnp.full((1, LANES), row_taps[tap], F32)
-        tap_ref[TAPS + tap : TAPS + tap + 1, :] = jnp.full((1, LANES), col_taps[tap], F32)
+        tap_ref[tap : tap + 1, :] = row_taps[tap]
+        tap_ref[TAPS + tap : TAPS + tap + 1, :] = col_taps[tap]
 
 
 def inner_resample(shifts, fractions, own, exponents):
     rows = own.shape[2]
     tiles = (rows // TILE) * (LANES // TILE)
     kept = rows - 2 * HALF_WIN
-    smem = pl.BlockSpec(memory_space=SMEM)
     vmem = pl.BlockSpec(memory_space=VMEM)
     return pl.pallas_call(
         inner_kernel,
@@ -170,13 +181,13 @@
             jax.ShapeDtypeStruct((2, LANES), jnp.int32),
             jax.ShapeDtypeStruct((2 * TAPS, LANES), F32),
         ),
-        in_specs=[smem] * 3 + [vmem] * 2,
+        in_specs=[vmem] * 4,
         out_specs=(vmem,) * 6,
         scratch_shapes=[VMEM((LANES // TILE, 2, kept, LANES), F32)],
         compiler_params=pltpu.CompilerParams(vmem_limit_bytes=LIMIT),
         cost_estimate=pl.CostEstimate(flops=2000000, bytes_accessed=2000000, transcendentals=0),
         name="inner_resample",
-    )(shifts, fractions, tap_table(), own, exponents)
+    )(shifts, fractions, own, exponents)
 
 
 def az_block():
@@ -285,7 +296,8 @@
     vector[0] = jnp.ones((dates, inner), F32)
     vector[1] = jnp.zeros((dates, inner), F32)
 
-    def iterate(_, carry):
+    def iterate(_, norms):
+        grown = []
         for half in range(2):
             cols = slice(half * HALF_TILE, (half + 1) * HALF_TILE)
             real, imag = vector[0, :, cols], vector[1, :, cols]
@@ -307,23 +319,23 @@
             new_real = factor * (total[:dates, left] - total[dates:, right]) + DAMP * real
             new_imag = factor * (total[:dates, right] + total[dates:, left]) + DAMP * imag
             square = jnp.sum(new_real * new_real + new_imag * new_imag, axis=0, keepdims=True)
-            inverse = lax.rsqrt(square / dates + EPS)
-            vector[0, :, cols] = new_real * inverse
-            vector[1, :, cols] = new_imag * inverse
-        return carry
-
-    lax.fori_loop(0, ITERS, iterate, 0)
+            grown.append(square / dates + EPS * norms[half])
+            vector[0, :, cols] = new_real
+            vector[1, :, cols] = new_imag
+        return tuple(grown)
+
+    norms = lax.fori_loop(0, ITERS, iterate, (jnp.ones((1, HALF_TILE), F32),) * 2)
+    inverse = lax.rsqrt(jnp.concatenate(norms, axis=1))
 
     def transform(real, imag, sign):
         high, low = split(jnp.concatenate([real, imag], axis=0))
         stacked = jnp.concatenate([high, low], axis=0)
-        cos = dot(stacked, transform_ref[0]) + dot(stacked, transform_ref[1])
-        sin = dot(stacked, transform_ref[2]) + dot(stacked, transform_ref[3])
-        cos = cos[:count] + cos[count:]
-        sin = sign * (sin[:count] + sin[count:])
+        cos, sin = dot(stacked, transform_ref[0]), dot(stacked, transform_ref[2])
+        cos = cos[:count] + cos[count:] + dot(high, transform_ref[1])
+        sin = sign * (sin[:count] + sin[count:] + dot(high, transform_ref[3]))
         return cos[:dates] - sin[dates:], sin[:dates] + cos[dates:]
 
-    spectrum_real, spectrum_imag = transform(vector[0], vector[1], 1.0)
+    spectrum_real, spectrum_imag = transform(vector[0] * inverse, vector[1] * inverse, 1.0)
     square_shape = (dates, dates)
     own = jnp.where(iota(square_shape, 0) == iota(square_shape, 1), exponent_ref[...], 0.0)
     exponent = jnp.sum(own, axis=1, keepdims=True)

time: 84.7 us -> 84.5 us (level)
  blocking collectives: 58 us -> 59.2 us
    all_to_all x1, blocking collectives: 39.4 us -> 40.6 us  [local(): lax.all_to_all(packed, 'date', split_axis=0, concat_axis=0, tiled=True)]
  transfers between devices with their start and end apart: 5 -> 5, of which waited for: 0 -> 0; matrix products, arithmetic and copies ran while one was open for 0% -> 0% of each run, Pallas kernels for 2% -> 1%
where the time goes in v5:
time: 84.5 us; the launch traced here: 84.2 us
  blocking collectives  59.2 us (70%)
  starting transfers between devices  18.1 us (21%)
  Pallas kernels  5.84 us (7%)
    all_to_all x1, blocking collectives, local(): lax.all_to_all(packed, 'date', split_axis=0, concat_axis=0, tiled=True)  40.6 us
    all_to_all x1, blocking collectives, local(): lax.all_to_all(filtered, 'date', split_axis=0, concat_axis=0, tiled=True)  18.6 us
    ppermute x5, starting transfers between devices, move(): return lax.ppermute(value, ('date', 'az'), pairs)  18.1 us
    pallas_call x1, Pallas kernels, link(): pl.pallas_call(link_kernel, out_shape=jax.ShapeDtypeStruct((dates, 2 * in...  3.42 us
  transfers between devices with their start and end apart: 5, of which 0 were waited for; matrix products, arithmetic and copies ran while one was open for 0% of the time, Pallas kernels for 1%

profile of v5, /device:TPU:7, one launch (start us, length us, event | category | flops | bytes accessed | tf_op | source)
XLA Modules:
  0.0 84.2 jit_solution(15453618778476959025)
XLA Ops:
  0.0 0.8 slice_select_fusion
  0.8 0.7 collective-permute-start
  1.5 0.0 collective-permute-done
  1.5 0.0 copy-start.2
  1.5 0.0 copy-start.3
  1.5 0.0 copy-start.4
  1.5 2.6 %collective-permute-start.1 = (f32[2,1,16,128]{3,2,1,0:T(8,128)S(1)}, f32[2,1,16,128]{3,2,1,0:T(8,128)S(1)}, u32[]{:S(2)}, u32[]{:S(2)}) collective-permute-start(f32[2,1,16,128]{3,2,1,0:T(8,128)S(1)} %get-tuple-element.16), channel_id=1, source_target_pairs={{0,1},{2,3},{5,6},{1,0},{3,2},{6,5},{8,9},{10,11},{13,14},{9,8},{1... | collective-permute-start | bytes 49160 | tf_op jit(solution)/shard_map/ppermute | solution.py:428
  4.1 13.6 %collective-permute-start.2 = (f32[2,1,16,128]{3,2,1,0:T(8,128)S(1)}, f32[2,1,16,128]{3,2,1,0:T(8,128)S(1)}, u32[]{:S(2)}, u32[]{:S(2)}) collective-permute-start(f32[2,1,16,128]{3,2,1,0:T(8,128)S(1)} %get-tuple-element.17), channel_id=1, source_target_pairs={{1,2},{3,4},{2,1},{4,3},{9,10},{11,12},{10,9},{12,11},{17,18},{19,... | collective-permute-start | bytes 49160 | tf_op jit(solution)/shard_map/ppermute | solution.py:428
  17.7 0.7 collective-permute-start.3
  18.3 0.7 collective-permute-start.4
  19.0 0.0 copy-done
  19.0 0.0 copy-done.2
  19.0 0.0 copy-done.3
  19.1 1.0 %inner_resample.1 = (bf16[64,16,128]{2,1,0:T(8,128)(2,1)S(1)}, f32[2,8,2,16,128]{4,3,2,1,0:T(8,128)S(1)}, bf16[768,128]{1,0:T(8,128)(2,1)S(1)}, f32[1,64]{1,0:T(...) custom-call(s32[1,2]{1,0:T(1,128)S(1)} %copy-done.2, s32[1,2]{1,0:T(1,128)S(1)} %copy-done.3, ...), custom_call_target="tpu_custom_call" | custom-call | flops 2000000 | bytes 2000000 | tf_op jit(solution)/shard_map/inner_resample/pallas_call | solution.py:174
  20.1 0.0 collective-permute-done.1.refs_3_
  20.1 0.0 collective-permute-done.2.refs_4_
  20.1 0.0 collective-permute-done.3.refs_5_
  20.1 0.0 collective-permute-done.4.refs_6_
  20.1 0.0 copy-start.1
  20.1 0.5 edge_resample.1
  20.6 40.6 %all_to_all.10.tile_ref = bf16[64,16,128]{2,1,0:T(8,128)(2,1)S(1)} all-to-all(bf16[64,16,128]{2,1,0:T(8,128)(2,1)S(1)} %edge_resample.1), channel_id=1, replica_groups=mesh['date'=64,'az'=8] {'date'}, dimensions={0} | all-to-all | bytes 524288 | tf_op jit(solution)/shard_map/all_to_all | solution.py:453
  61.3 3.4 %link.1 = bf16[64,512]{1,0:T(8,128)(2,1)S(1)} custom-call(bf16[64,16,128]{2,1,0:T(8,128)(2,1)S(1)} %all_to_all.10.tile_ref, f32[1,64]{1,0:T(1,128)S(1)} %get-tuple-element.21.exponent_ref, bf16[4,256,256]{2,1,0:T(8,128)(2,1)S(1)} %copy-done.1, bf16[768,128]{1,0:T(8,128)(2,1)S(1)} %get-tuple-element.22.mask), custom_call_target="tpu_custom_call" | custom-call | tf_op jit(solution)/shard_map/link/pallas_call | solution.py:354
  64.7 18.6 %all_to_all.11 = bf16[64,4,128]{2,1,0:T(4,128)(2,1)S(1)} all-to-all(bf16[64,4,128]{2,1,0:T(4,128)(2,1)S(1)} %reshape.10), channel_id=1, replica_groups=mesh['date'=64,'az'=8] {'date'}, dimensions={0} | all-to-all | bytes 131072 | tf_op jit(solution)/shard_map/all_to_all | solution.py:456
  83.3 0.9 %unpack.1 = f32[2,1,128,128]{3,2,1,0:T(8,128)} custom-call(bf16[64,512]{1,0:T(8,128)(2,1)S(1)} %bitcast.5), custom_call_target="tpu_custom_call" | custom-call | tf_op jit(solution)/shard_map/unpack/pallas_call | solution.py:398
  (5 shorter events, 0.0 us)
Async XLA Ops:
  0.0 19.0 %copy-start = (f32[2,1,128,128]{3,2,1,0:T(8,128)S(1)}, f32[2,1,128,128]{3,2,1,0:T(8,128)}, u32[]{:S(2)}) copy-start(f32[2,1,128,128]{3,2,1,0:T(8,128)} %refs_2_.1) | copy-start | bytes 393220
  0.8 0.7 collective-permute-start
  1.5 17.6 %copy-start.2 = (s32[1,2]{1,0:T(1,128)S(1)}, s32[1,2]{1,0:T(1,128)}, u32[]{:S(2)}) copy-start(s32[1,2]{1,0:T(1,128)} %shift_ref.1) | copy-start | bytes 28
  1.5 17.6 %copy-start.3 = (s32[1,2]{1,0:T(1,128)S(1)}, s32[1,2]{1,0:T(1,128)}, u32[]{:S(2)}) copy-start(s32[1,2]{1,0:T(1,128)} %fraction_ref.1) | copy-start | bytes 28
  1.5 17.6 %copy-start.4 = (f32[64]{0:T(128)S(1)}, f32[64]{0:T(128)}, u32[]{:S(2)}) copy-start(f32[64]{0:T(128)} %param.8) | copy-start | bytes 772
  1.5 18.6 %collective-permute-start.1 = (f32[2,1,16,128]{3,2,1,0:T(8,128)S(1)}, f32[2,1,16,128]{3,2,1,0:T(8,128)S(1)}, u32[]{:S(2)}, u32[]{:S(2)}) collective-permute-start(f32[2,1,16,128]{3,2,1,0:T(8,128)S(1)} %get-tuple-element.16), channel_id=1, source_target_pairs={{0,1},{2,3},{5,6},{1,0},{3,2},{6,5},{8,9},{10,11},{13,14},{9,8},{1... | collective-permute-start | bytes 49160 | tf_op jit(solution)/shard_map/ppermute | solution.py:428
  4.1 16.0 %collective-permute-start.2 = (f32[2,1,16,128]{3,2,1,0:T(8,128)S(1)}, f32[2,1,16,128]{3,2,1,0:T(8,128)S(1)}, u32[]{:S(2)}, u32[]{:S(2)}) collective-permute-start(f32[2,1,16,128]{3,2,1,0:T(8,128)S(1)} %get-tuple-element.17), channel_id=1, source_target_pairs={{1,2},{3,4},{2,1},{4,3},{9,10},{11,12},{10,9},{12,11},{17,18},{19,... | collective-permute-start | bytes 49160 | tf_op jit(solution)/shard_map/ppermute | solution.py:428
  17.7 2.4 %collective-permute-start.3 = (f32[2,1,16,128]{3,2,1,0:T(8,128)S(1)}, f32[2,1,16,128]{3,2,1,0:T(8,128)S(1)}, u32[]{:S(2)}, u32[]{:S(2)}) collective-permute-start(f32[2,1,16,128]{3,2,1,0:T(8,128)S(1)} %get-tuple-element.18), channel_id=1, source_target_pairs={{4,5},{6,7},{5,4},{7,6},{12,13},{14,15},{13,12},{15,14},{20,21},{2... | collective-permute-start | bytes 49160 | tf_op jit(solution)/shard_map/ppermute | solution.py:428
  18.3 1.8 %collective-permute-start.4 = (f32[2,1,16,128]{3,2,1,0:T(8,128)S(1)}, f32[2,1,16,128]{3,2,1,0:T(8,128)S(1)}, u32[]{:S(2)}, u32[]{:S(2)}) collective-permute-start(f32[2,1,16,128]{3,2,1,0:T(8,128)S(1)} %collective-permute-done), channel_id=1, source_target_pairs={{0,259},{8,267},{16,275},{24,283},{32,291},{40,299},{48,307},{56,3... | collective-permute-start | bytes 49160 | tf_op jit(solution)/shard_map/ppermute | solution.py:428
  20.1 41.1 %copy-start.1 = (bf16[4,256,256]{2,1,0:T(8,128)(2,1)S(1)}, bf16[4,256,256]{2,1,0:T(8,128)(2,1)}, u32[]{:S(2)}) copy-start(bf16[4,256,256]{2,1,0:T(8,128)(2,1)} %constant.14.clone.transform_ref) | copy-start | bytes 1572868

commit v6 on v5

--- a/solution.py
+++ b/solution.py
@@ -368,14 +368,15 @@
     )(tile, exponents, patch_transform(), mask)
 
 
-def unpack_kernel(tile_ref, out_ref):
+def unpack_kernel(tile_ref, out_ref, stage, sems):
     tile_cols = LANES // TILE
     shape = (8, LANES)
     sub = iota(shape, 0)
     column = iota(shape, 1) // TILE
     halves = TILE // 8
-    for tile_row in range(tile_ref.shape[0] // tile_cols):
-        for plane in range(2):
+    copies = []
+    for plane in range(2):
+        for tile_row in range(tile_ref.shape[0] // tile_cols):
             for half in range(halves):
                 first = (plane * halves + half) * LANES
                 value = tile_ref[
@@ -389,17 +390,22 @@
                     swapped = jnp.where(sub_bit, behind, ahead)
                     value = jnp.where(sub_bit == col_bit, value, swapped)
                 row = tile_row * TILE + half * 8
-                out_ref[plane, 0, row : row + 8, :] = value
+                stage[plane, 0, row : row + 8, :] = value
+        copies.append(pltpu.make_async_copy(stage.at[plane], out_ref.at[plane], sems.at[plane]))
+        copies[-1].start()
+    for copy in copies:
+        copy.wait()
 
 
 def unpack(tiles):
     rows = tiles.shape[0] * TILE * TILE // LANES
-    vmem = pl.BlockSpec(memory_space=VMEM)
+    shape = (2, 1, rows, LANES)
     return pl.pallas_call(
         unpack_kernel,
-        out_shape=jax.ShapeDtypeStruct((2, 1, rows, LANES), F32),
-        in_specs=[vmem],
-        out_specs=vmem,
+        out_shape=jax.ShapeDtypeStruct(shape, F32),
+        in_specs=[pl.BlockSpec(memory_space=VMEM)],
+        out_specs=pl.BlockSpec(memory_space=pl.ANY),
+        scratch_shapes=[VMEM(shape, F32), pltpu.SemaphoreType.DMA((2,))],
         compiler_params=pltpu.CompilerParams(vmem_limit_bytes=LIMIT),
         name="unpack",
     )(tiles)

time: 84.5 us -> 84.5 us (level)
  no operation moved by 1% of the time
where the time goes in v6:
time: 84.5 us; the launch traced here: 84.2 us
  blocking collectives  59.2 us (70%)
  starting transfers between devices  18.1 us (21%)
  Pallas kernels  5.83 us (7%)
    all_to_all x1, blocking collectives, local(): lax.all_to_all(packed, 'date', split_axis=0, concat_axis=0, tiled=True)  40.6 us
    all_to_all x1, blocking collectives, local(): lax.all_to_all(filtered, 'date', split_axis=0, concat_axis=0, tiled=True)  18.6 us
    ppermute x5, starting transfers between devices, move(): return lax.ppermute(value, ('date', 'az'), pairs)  18.1 us
    pallas_call x1, Pallas kernels, link(): pl.pallas_call(link_kernel, out_shape=jax.ShapeDtypeStruct((dates, 2 * in...  3.42 us
  transfers between devices with their start and end apart: 5, of which 0 were waited for; matrix products, arithmetic and copies ran while one was open for 0% of the time, Pallas kernels for 1%

profile of v6, /device:TPU:7, one launch (start us, length us, event | category | flops | bytes accessed | tf_op | source)
XLA Modules:
  0.0 84.2 jit_solution(13300140312779899560)
XLA Ops:
  0.0 0.8 slice_select_fusion
  0.8 0.7 collective-permute-start
  1.5 0.0 collective-permute-done
  1.5 0.0 copy-start.2
  1.5 0.0 copy-start.3
  1.5 0.0 copy-start.4
  1.5 2.6 %collective-permute-start.1 = (f32[2,1,16,128]{3,2,1,0:T(8,128)S(1)}, f32[2,1,16,128]{3,2,1,0:T(8,128)S(1)}, u32[]{:S(2)}, u32[]{:S(2)}) collective-permute-start(f32[2,1,16,128]{3,2,1,0:T(8,128)S(1)} %get-tuple-element.16), channel_id=1, source_target_pairs={{0,1},{2,3},{5,6},{1,0},{3,2},{6,5},{8,9},{10,11},{13,14},{9,8},{1... | collective-permute-start | bytes 49160 | tf_op jit(solution)/shard_map/ppermute | solution.py:434
  4.1 13.6 %collective-permute-start.2 = (f32[2,1,16,128]{3,2,1,0:T(8,128)S(1)}, f32[2,1,16,128]{3,2,1,0:T(8,128)S(1)}, u32[]{:S(2)}, u32[]{:S(2)}) collective-permute-start(f32[2,1,16,128]{3,2,1,0:T(8,128)S(1)} %get-tuple-element.17), channel_id=1, source_target_pairs={{1,2},{3,4},{2,1},{4,3},{9,10},{11,12},{10,9},{12,11},{17,18},{19,... | collective-permute-start | bytes 49160 | tf_op jit(solution)/shard_map/ppermute | solution.py:434
  17.7 0.7 collective-permute-start.3
  18.3 0.7 collective-permute-start.4
  19.0 0.0 copy-done
  19.0 0.0 copy-done.2
  19.0 0.0 copy-done.3
  19.1 1.0 %inner_resample.1 = (bf16[64,16,128]{2,1,0:T(8,128)(2,1)S(1)}, f32[2,8,2,16,128]{4,3,2,1,0:T(8,128)S(1)}, bf16[768,128]{1,0:T(8,128)(2,1)S(1)}, f32[1,64]{1,0:T(...) custom-call(s32[1,2]{1,0:T(1,128)S(1)} %copy-done.2, s32[1,2]{1,0:T(1,128)S(1)} %copy-done.3, ...), custom_call_target="tpu_custom_call" | custom-call | flops 2000000 | bytes 2000000 | tf_op jit(solution)/shard_map/inner_resample/pallas_call | solution.py:174
  20.1 0.0 collective-permute-done.1.refs_3_
  20.1 0.0 collective-permute-done.2.refs_4_
  20.1 0.0 collective-permute-done.3.refs_5_
  20.1 0.0 collective-permute-done.4.refs_6_
  20.1 0.0 copy-start.1
  20.1 0.5 edge_resample.1
  20.6 40.6 %all_to_all.10.tile_ref = bf16[64,16,128]{2,1,0:T(8,128)(2,1)S(1)} all-to-all(bf16[64,16,128]{2,1,0:T(8,128)(2,1)S(1)} %edge_resample.1), channel_id=1, replica_groups=mesh['date'=64,'az'=8] {'date'}, dimensions={0} | all-to-all | bytes 524288 | tf_op jit(solution)/shard_map/all_to_all | solution.py:459
  61.3 3.4 %link.1 = bf16[64,512]{1,0:T(8,128)(2,1)S(1)} custom-call(bf16[64,16,128]{2,1,0:T(8,128)(2,1)S(1)} %all_to_all.10.tile_ref, f32[1,64]{1,0:T(1,128)S(1)} %get-tuple-element.21.exponent_ref, bf16[4,256,256]{2,1,0:T(8,128)(2,1)S(1)} %copy-done.1, bf16[768,128]{1,0:T(8,128)(2,1)S(1)} %get-tuple-element.22.mask), custom_call_target="tpu_custom_call" | custom-call | tf_op jit(solution)/shard_map/link/pallas_call | solution.py:354
  64.7 18.6 %all_to_all.11 = bf16[64,4,128]{2,1,0:T(4,128)(2,1)S(1)} all-to-all(bf16[64,4,128]{2,1,0:T(4,128)(2,1)S(1)} %reshape.10), channel_id=1, replica_groups=mesh['date'=64,'az'=8] {'date'}, dimensions={0} | all-to-all | bytes 131072 | tf_op jit(solution)/shard_map/all_to_all | solution.py:462
  83.3 0.9 %unpack.1 = f32[2,1,128,128]{3,2,1,0:T(8,128)} custom-call(bf16[64,512]{1,0:T(8,128)(2,1)S(1)} %bitcast.5), custom_call_target="tpu_custom_call" | custom-call | tf_op jit(solution)/shard_map/unpack/pallas_call | solution.py:403
  (5 shorter events, 0.0 us)
Async XLA Ops:
  0.0 19.0 %copy-start = (f32[2,1,128,128]{3,2,1,0:T(8,128)S(1)}, f32[2,1,128,128]{3,2,1,0:T(8,128)}, u32[]{:S(2)}) copy-start(f32[2,1,128,128]{3,2,1,0:T(8,128)} %refs_2_.1) | copy-start | bytes 393220
  0.8 0.7 collective-permute-start
  1.5 17.6 %copy-start.2 = (s32[1,2]{1,0:T(1,128)S(1)}, s32[1,2]{1,0:T(1,128)}, u32[]{:S(2)}) copy-start(s32[1,2]{1,0:T(1,128)} %shift_ref.1) | copy-start | bytes 28
  1.5 17.6 %copy-start.3 = (s32[1,2]{1,0:T(1,128)S(1)}, s32[1,2]{1,0:T(1,128)}, u32[]{:S(2)}) copy-start(s32[1,2]{1,0:T(1,128)} %fraction_ref.1) | copy-start | bytes 28
  1.5 17.6 %copy-start.4 = (f32[64]{0:T(128)S(1)}, f32[64]{0:T(128)}, u32[]{:S(2)}) copy-start(f32[64]{0:T(128)} %param.8) | copy-start | bytes 772
  1.5 18.6 %collective-permute-start.1 = (f32[2,1,16,128]{3,2,1,0:T(8,128)S(1)}, f32[2,1,16,128]{3,2,1,0:T(8,128)S(1)}, u32[]{:S(2)}, u32[]{:S(2)}) collective-permute-start(f32[2,1,16,128]{3,2,1,0:T(8,128)S(1)} %get-tuple-element.16), channel_id=1, source_target_pairs={{0,1},{2,3},{5,6},{1,0},{3,2},{6,5},{8,9},{10,11},{13,14},{9,8},{1... | collective-permute-start | bytes 49160 | tf_op jit(solution)/shard_map/ppermute | solution.py:434
  4.1 16.0 %collective-permute-start.2 = (f32[2,1,16,128]{3,2,1,0:T(8,128)S(1)}, f32[2,1,16,128]{3,2,1,0:T(8,128)S(1)}, u32[]{:S(2)}, u32[]{:S(2)}) collective-permute-start(f32[2,1,16,128]{3,2,1,0:T(8,128)S(1)} %get-tuple-element.17), channel_id=1, source_target_pairs={{1,2},{3,4},{2,1},{4,3},{9,10},{11,12},{10,9},{12,11},{17,18},{19,... | collective-permute-start | bytes 49160 | tf_op jit(solution)/shard_map/ppermute | solution.py:434
  17.7 2.4 %collective-permute-start.3 = (f32[2,1,16,128]{3,2,1,0:T(8,128)S(1)}, f32[2,1,16,128]{3,2,1,0:T(8,128)S(1)}, u32[]{:S(2)}, u32[]{:S(2)}) collective-permute-start(f32[2,1,16,128]{3,2,1,0:T(8,128)S(1)} %get-tuple-element.18), channel_id=1, source_target_pairs={{4,5},{6,7},{5,4},{7,6},{12,13},{14,15},{13,12},{15,14},{20,21},{2... | collective-permute-start | bytes 49160 | tf_op jit(solution)/shard_map/ppermute | solution.py:434
  18.3 1.8 %collective-permute-start.4 = (f32[2,1,16,128]{3,2,1,0:T(8,128)S(1)}, f32[2,1,16,128]{3,2,1,0:T(8,128)S(1)}, u32[]{:S(2)}, u32[]{:S(2)}) collective-permute-start(f32[2,1,16,128]{3,2,1,0:T(8,128)S(1)} %collective-permute-done), channel_id=1, source_target_pairs={{0,259},{8,267},{16,275},{24,283},{32,291},{40,299},{48,307},{56,3... | collective-permute-start | bytes 49160 | tf_op jit(solution)/shard_map/ppermute | solution.py:434
  20.1 41.1 %copy-start.1 = (bf16[4,256,256]{2,1,0:T(8,128)(2,1)S(1)}, bf16[4,256,256]{2,1,0:T(8,128)(2,1)}, u32[]{:S(2)}) copy-start(bf16[4,256,256]{2,1,0:T(8,128)(2,1)} %constant.14.clone.transform_ref) | copy-start | bytes 1572868
